TPU v7x, 32 devices: a whole 2x2x4 slice. The times are simulated.
32 devices in a mesh: tile: 2 (over x), gx: 16 (over z, y, core).
Axes of the slice: x: 2, y: 2, z: 4, core: 2. Of those that a mesh axis runs over, the one named last changes fastest.
Arguments:
- points: bfloat16 [524288, 192], P(('tile', 'gx')), parts along dimension 0, may hold values from -6 to 6
- gain: float32 [192], replicated, may hold values from 0.1 to 1.9
- w_qkv: bfloat16 [192, 576], replicated
- w_out: bfloat16 [192, 192], replicated, may hold values from -1.75 to 1.75
- counts: int32 [4096], P(('tile', 'gx')), parts along dimension 0, may hold values from 32 to 128, as said below
- far_index: int32 [4096, 128], P(('tile', 'gx')), parts along dimension 0, may hold values from 0 to 2175, as said below
Outputs:
- attended: bfloat16 [524288, 192], P(('tile', 'gx')), parts along dimension 0
There are 2 independent parts, one for each index of `tile`. A program takes and returns all parts, laid end to end along the dimension named above; an argument that names none is the same for every part. Nothing has to cross between parts.
Inputs may be any that keep to these rules, and one draw needn't show every extreme that they name: `counts`: every window of a tile has between 32 and 128 live points and some window has exactly 128. w * 128 - 1024 + far_index[w, :] names live point slots of windows whose rows lie within 1024 rows before the start or after the end of window w, inside the tile.
All inputs are finite; a program needn't handle non-finite values.
Results may differ from a plain program's by a relative error of at most 0.002.
The roundings to bfloat16 on the way count: a program that leaves them out, or rounds other values in their place, can miss the bound.
Values may be sent and summed in bfloat16 or wider, within the bound.
No kernel may reach another device: no remote copies, remote signals or barrier semaphores. Data moves between devices by JAX's collectives and lax.ppermute only.
A program may use at most 192 MiB of HBM per device.

v0:
```python
import math

import jax
import jax.numpy as jnp
from jax import lax
from jax.sharding import PartitionSpec as P

HEADS = 6
WIN = 128
REACH = 1024


def extended_2(block, sides, width):
    for axis, dim in sides:
        count = lax.axis_size(axis)
        forward = [(i, i + 1) for i in range(count - 1)]
        backward = [(target, source) for source, target in forward]
        low = lax.ppermute(
            lax.slice_in_dim(block, block.shape[dim] - width, None, axis=dim), axis, forward
        )
        high = lax.ppermute(lax.slice_in_dim(block, 0, width, axis=dim), axis, backward)
        block = jnp.concatenate([low, block, high], axis=dim)
    return block


def attend_windows(queries, dense_kv, far_kv, live):
    group, slots, width = queries.shape
    head_dim = width // HEADS
    far_count = far_kv.shape[1]
    qh = queries.reshape(group, slots, HEADS, head_dim)
    allkv = jnp.concatenate([dense_kv, far_kv], axis=1)
    keys = allkv[..., :width].reshape(group, slots + far_count, HEADS, head_dim)
    values = allkv[..., width:].reshape(group, slots + far_count, HEADS, head_dim)
    scores = jnp.einsum(
        "gqhd,gkhd->ghqk", qh, keys, preferred_element_type=jnp.float32
    ) / math.sqrt(head_dim)
    valid = jnp.concatenate(
        [jnp.arange(slots)[None, :] < live[:, None], jnp.ones((group, far_count), bool)], axis=1
    )
    scores = jnp.where(valid[:, None, None, :], scores, jnp.float32(-1e30))
    top = jnp.max(scores, axis=-1, keepdims=True)
    expo = jnp.exp(scores - top)
    prob = (expo / jnp.sum(expo, axis=-1, keepdims=True)).astype(jnp.bfloat16)
    mixed = jnp.einsum("ghqk,gkhd->gqhd", prob, values, preferred_element_type=jnp.float32)
    return mixed.reshape(group, slots, width).astype(jnp.bfloat16)


def shards(points, gain, w_qkv, w_out, counts, far_index):
    rows, width = points.shape
    xf = points.astype(jnp.float32)
    mean = jnp.mean(xf, axis=1, keepdims=True)
    var = jnp.mean((xf - mean) ** 2, axis=1, keepdims=True)
    normed = ((xf - mean) / jnp.sqrt(var + 1e-05) * gain).astype(jnp.bfloat16)
    qkv = jnp.dot(normed, w_qkv, preferred_element_type=jnp.float32).astype(jnp.bfloat16)
    queries = qkv[:, :width]
    keyvals = qkv[:, width:]
    extended = extended_2(keyvals, (("gx", 0),), REACH)
    far_count = far_index.shape[1]
    windows = rows // WIN
    starts = jnp.arange(windows, dtype=jnp.int32) * WIN
    local_index = (far_index + starts[:, None]).reshape(windows * far_count)
    far_rows = jnp.take(extended, local_index, axis=0, mode="clip")
    group = math.gcd(windows, 16)
    blocks = windows // group
    q4 = queries.reshape(blocks, group, WIN, width)
    kv4 = keyvals.reshape(blocks, group, WIN, 2 * width)
    far4 = far_rows.reshape(blocks, group, far_count, 2 * width)
    live = counts.reshape(blocks, group)

    def one_block(items):
        qb, kvb, fb, lb = items
        return attend_windows(qb, kvb, fb, lb)

    mixed = lax.map(one_block, (q4, kv4, far4, live)).reshape(rows, width)
    return jnp.dot(mixed, w_out, preferred_element_type=jnp.float32).astype(jnp.bfloat16)


def solution(mesh):
    return jax.shard_map(
        shards,
        mesh=mesh,
        in_specs=(
            P(("tile", "gx"), None),
            P(),
            P(),
            P(),
            P(("tile", "gx")),
            P(("tile", "gx"), None),
        ),
        out_specs=P(("tile", "gx"), None),
        check_vma=False,
    )
```

profile of v0, /device:TPU:1, one launch (start us, length us, event | category | flops | bytes accessed | tf_op | source)
XLA Modules:
  0.0 379.0 jit_solution(5004375237657870303)
XLA Ops:
  0.0 3.9 %convert_reduce_fusion = f32[16384]{0:T(1024)S(1)} fusion(bf16[16384,192]{0,1:T(8,128)(2,1)} %param.8), kind=kLoop, calls=%fused_computation.29 | loop fusion | flops 6275072 | bytes 6356992 | tf_op jit(solution)/shard_map/reduce_sum | solution.py:51
  4.6 1.7 fusion.15
  6.4 9.3 %convolution_convert_fusion = bf16[16384,576]{0,1:T(8,128)(2,1)} fusion(bf16[192,576]{1,0:T(8,128)(2,1)S(1)} %copy-done, bf16[16384,192]{0,1:T(8,128)(2,1)S(1)} %copy-done.3, f32[192]{0:T(256)S(1)} %copy-done.7, f32[16384]{0:T(1024)S(1)} %add_sqrt_fusion, f32[16384]{0:T(1024)S(1)} %broadcast_multiply_fusion), kind=kOutput, calls=%fused_computation.26 | convolution fusion | flops 3649044480 | bytes 25518848 | tf_op jit(solution)/shard_map/dot_general | solution.py:54
  17.2 4.5 %collective-permute-start = (bf16[1024,384]{0,1:T(8,128)(2,1)S(1)}, bf16[1024,384]{0,1:T(8,128)(2,1)S(1)}, u32[]{:S(2)}, u32[]{:S(2)}) collective-permute-start(bf16[1024,384]{0,1:T(8,128)(2,1)S(1)} %get-tuple-element.66), channel_id=1, source_target_pairs={{0,1},{1,2},{2,3},{3,4},{4,5},{5,6},{6,7},{7,8},{8,9},{9,10},{10,1... | collective-permute-start | bytes 2359304 | tf_op jit(solution)/shard_map/ppermute | solution.py:18
  21.8 1.9 collective-permute-start.1
  23.7 14.4 %fusion.26 = (bf16[16384,384]{0,1:T(8,128)(2,1)}, bf16[48,8,128,128]{3,1,2,0:T(8,128)(2,1)}) fusion(bf16[16384,576]{0,1:T(8,128)(2,1)} %convolution_convert_fusion), kind=kLoop, calls=%fused_computation.49 | loop fusion | bytes 37748736 | tf_op jit(solution)/shard_map/slice | solution.py:56
  38.1 6.1 %slice_bitcast_fusion = bf16[24,8,128,128]{3,1,2,0:T(8,128)(2,1)} fusion(bf16[16384,576]{0,1:T(8,128)(2,1)} %convolution_convert_fusion), kind=kLoop, calls=%fused_computation.38 | loop fusion | bytes 12582912
  44.3 7.6 %copy.22 = bf16[24,8,128,128]{3,2,1,0:T(8,128)(2,1)} copy(bf16[24,8,128,128]{3,1,2,0:T(8,128)(2,1)} %slice_bitcast_fusion) | data formatting | bytes 12582912
  52.1 6.7 %copy.21 = bf16[48,8,128,128]{3,2,1,0:T(8,128)(2,1)} copy(bf16[48,8,128,128]{3,1,2,0:T(8,128)(2,1)S(1)} %copy-done.2) | data formatting | bytes 25165824
  60.8 7.4 %pad_maximum_fusion.1 = bf16[18432,384]{0,1:T(8,128)(2,1)} fusion(bf16[1024,384]{0,1:T(8,128)(2,1)S(1)} %collective-permute-done.1, bf16[16384,384]{0,1:T(8,128)(2,1)S(1)} %bitcast.64, bf16[1024,384]{0,1:T(8,128)(2,1)S(1)} %collective-permute-done), kind=kLoop, calls=%fused_computation.32 | loop fusion | flops 42467328 | bytes 28311552 | tf_op jit(solution)/shard_map/concatenate | solution.py:22
  68.3 18.5 %copy.11 = bf16[18432,384]{1,0:T(8,128)(2,1)} copy(bf16[18432,384]{0,1:T(8,128)(2,1)} %pad_maximum_fusion.1) | data formatting | bytes 28311552 | tf_op jit(solution)/shard_map/concatenate | solution.py:22
  86.8 70.7 %gather_fusion = bf16[16384,384]{1,0:T(8,128)(2,1)} fusion(bf16[18432,384]{1,0:T(8,128)(2,1)} %copy.11, s32[16384]{0:T(1024)S(1)} %bitcast_clamp_fusion), kind=kCustom, calls=%fused_computation | custom fusion | bytes 25231360 | tf_op jit(solution)/shard_map/jit(_take)/gather | solution.py:62
  157.5 211.4 %while.10 = (s32[]{:T(128)}, bf16[8,16,128,192]{2,1,0,3:T(8,128)(2,1)}, bf16[8,16,128,384]{2,1,0,3:T(8,128)(2,1)}, bf16[8,16,128,384]{3,2,1,0:T(8,128)(2,1)}, s3...) while((s32[]{:T(128)}, bf16[8,16,128,192]{2,1,0,3:T(8,128)(2,1)}, ...), condition=%wide.region_5.6_spmd, body=%wide.region_2.5_spmd.sunk | while | flops 428214528 | bytes 53588272 | solution.py:74
  160.0 1.6 constant_dynamic-slice_fusion.7
  162.6 1.7 constant_dynamic-slice_fusion.8
  166.3 10.3 %fusion.44 = (f32[16,6,128]{2,1,0:T(8,128)S(1)}, f32[16,6,128,256]{3,2,1,0:T(8,128)}) fusion(pred[16,256]{1,0:T(8,128)(4,1)S(1)} %concatenate.11, bf16[16,128,6,32]{1,3,2,0:T(8,128)(2,1)} %bitcast.69, bf16[16,256,6,32]{1,3,2,0:T(8,128)(2,1)} %bitcast.66), kind=kOutput, calls=%fused_computation.47.clone.1 | convolution fusion | flops 213909760 | bytes 14995456 | tf_op jit(solution)/shard_map/while/body/eval_jaxpr/sub | solution.py:42
  176.6 5.9 %fusion.45 = bf16[16,6,32,128]{3,2,1,0:T(8,128)(2,1)S(1)} fusion(bf16[16,256,6,32]{1,3,2,0:T(8,128)(2,1)S(1)} %bitcast.65, f32[16,6,128,256]{3,2,1,0:T(8,128)} %get-tuple-element.113, f32[16,6,128]{2,1,0:T(8,128)S(1)} %get-tuple-element.114), kind=kOutput, calls=%fused_computation.15.clone.1 | convolution fusion | flops 208011264 | bytes 14991360 | tf_op jit(solution)/shard_map/while/body/eval_jaxpr/ghqk,gkhd->gqhd/dot_general | solution.py:44
  186.5 1.6 constant_dynamic-slice_fusion.7
  189.0 1.7 constant_dynamic-slice_fusion.8
  191.2 1.5 pad_maximum_fusion.3
  192.7 10.3 %fusion.44 = (f32[16,6,128]{2,1,0:T(8,128)S(1)}, f32[16,6,128,256]{3,2,1,0:T(8,128)}) fusion(pred[16,256]{1,0:T(8,128)(4,1)S(1)} %concatenate.11, bf16[16,128,6,32]{1,3,2,0:T(8,128)(2,1)} %bitcast.69, bf16[16,256,6,32]{1,3,2,0:T(8,128)(2,1)} %bitcast.66), kind=kOutput, calls=%fused_computation.47.clone.1 | convolution fusion | flops 213909760 | bytes 14995456 | tf_op jit(solution)/shard_map/while/body/eval_jaxpr/sub | solution.py:42
  203.0 5.9 %fusion.45 = bf16[16,6,32,128]{3,2,1,0:T(8,128)(2,1)S(1)} fusion(bf16[16,256,6,32]{1,3,2,0:T(8,128)(2,1)S(1)} %bitcast.65, f32[16,6,128,256]{3,2,1,0:T(8,128)} %get-tuple-element.113, f32[16,6,128]{2,1,0:T(8,128)S(1)} %get-tuple-element.114), kind=kOutput, calls=%fused_computation.15.clone.1 | convolution fusion | flops 208011264 | bytes 14991360 | tf_op jit(solution)/shard_map/while/body/eval_jaxpr/ghqk,gkhd->gqhd/dot_general | solution.py:44
  212.9 1.6 constant_dynamic-slice_fusion.7
  215.4 1.7 constant_dynamic-slice_fusion.8
  217.6 1.5 pad_maximum_fusion.3
  219.1 10.3 %fusion.44 = (f32[16,6,128]{2,1,0:T(8,128)S(1)}, f32[16,6,128,256]{3,2,1,0:T(8,128)}) fusion(pred[16,256]{1,0:T(8,128)(4,1)S(1)} %concatenate.11, bf16[16,128,6,32]{1,3,2,0:T(8,128)(2,1)} %bitcast.69, bf16[16,256,6,32]{1,3,2,0:T(8,128)(2,1)} %bitcast.66), kind=kOutput, calls=%fused_computation.47.clone.1 | convolution fusion | flops 213909760 | bytes 14995456 | tf_op jit(solution)/shard_map/while/body/eval_jaxpr/sub | solution.py:42
  229.4 5.9 %fusion.45 = bf16[16,6,32,128]{3,2,1,0:T(8,128)(2,1)S(1)} fusion(bf16[16,256,6,32]{1,3,2,0:T(8,128)(2,1)S(1)} %bitcast.65, f32[16,6,128,256]{3,2,1,0:T(8,128)} %get-tuple-element.113, f32[16,6,128]{2,1,0:T(8,128)S(1)} %get-tuple-element.114), kind=kOutput, calls=%fused_computation.15.clone.1 | convolution fusion | flops 208011264 | bytes 14991360 | tf_op jit(solution)/shard_map/while/body/eval_jaxpr/ghqk,gkhd->gqhd/dot_general | solution.py:44
  239.3 1.6 constant_dynamic-slice_fusion.7
  241.8 1.7 constant_dynamic-slice_fusion.8
  245.5 10.3 %fusion.44 = (f32[16,6,128]{2,1,0:T(8,128)S(1)}, f32[16,6,128,256]{3,2,1,0:T(8,128)}) fusion(pred[16,256]{1,0:T(8,128)(4,1)S(1)} %concatenate.11, bf16[16,128,6,32]{1,3,2,0:T(8,128)(2,1)} %bitcast.69, bf16[16,256,6,32]{1,3,2,0:T(8,128)(2,1)} %bitcast.66), kind=kOutput, calls=%fused_computation.47.clone.1 | convolution fusion | flops 213909760 | bytes 14995456 | tf_op jit(solution)/shard_map/while/body/eval_jaxpr/sub | solution.py:42
  255.8 5.9 %fusion.45 = bf16[16,6,32,128]{3,2,1,0:T(8,128)(2,1)S(1)} fusion(bf16[16,256,6,32]{1,3,2,0:T(8,128)(2,1)S(1)} %bitcast.65, f32[16,6,128,256]{3,2,1,0:T(8,128)} %get-tuple-element.113, f32[16,6,128]{2,1,0:T(8,128)S(1)} %get-tuple-element.114), kind=kOutput, calls=%fused_computation.15.clone.1 | convolution fusion | flops 208011264 | bytes 14991360 | tf_op jit(solution)/shard_map/while/body/eval_jaxpr/ghqk,gkhd->gqhd/dot_general | solution.py:44
  265.7 1.6 constant_dynamic-slice_fusion.7
  268.3 1.7 constant_dynamic-slice_fusion.8
  271.9 10.3 %fusion.44 = (f32[16,6,128]{2,1,0:T(8,128)S(1)}, f32[16,6,128,256]{3,2,1,0:T(8,128)}) fusion(pred[16,256]{1,0:T(8,128)(4,1)S(1)} %concatenate.11, bf16[16,128,6,32]{1,3,2,0:T(8,128)(2,1)} %bitcast.69, bf16[16,256,6,32]{1,3,2,0:T(8,128)(2,1)} %bitcast.66), kind=kOutput, calls=%fused_computation.47.clone.1 | convolution fusion | flops 213909760 | bytes 14995456 | tf_op jit(solution)/shard_map/while/body/eval_jaxpr/sub | solution.py:42
  282.3 5.9 %fusion.45 = bf16[16,6,32,128]{3,2,1,0:T(8,128)(2,1)S(1)} fusion(bf16[16,256,6,32]{1,3,2,0:T(8,128)(2,1)S(1)} %bitcast.65, f32[16,6,128,256]{3,2,1,0:T(8,128)} %get-tuple-element.113, f32[16,6,128]{2,1,0:T(8,128)S(1)} %get-tuple-element.114), kind=kOutput, calls=%fused_computation.15.clone.1 | convolution fusion | flops 208011264 | bytes 14991360 | tf_op jit(solution)/shard_map/while/body/eval_jaxpr/ghqk,gkhd->gqhd/dot_general | solution.py:44
  292.1 1.6 constant_dynamic-slice_fusion.7
  294.7 1.7 constant_dynamic-slice_fusion.8
  298.4 10.3 %fusion.44 = (f32[16,6,128]{2,1,0:T(8,128)S(1)}, f32[16,6,128,256]{3,2,1,0:T(8,128)}) fusion(pred[16,256]{1,0:T(8,128)(4,1)S(1)} %concatenate.11, bf16[16,128,6,32]{1,3,2,0:T(8,128)(2,1)} %bitcast.69, bf16[16,256,6,32]{1,3,2,0:T(8,128)(2,1)} %bitcast.66), kind=kOutput, calls=%fused_computation.47.clone.1 | convolution fusion | flops 213909760 | bytes 14995456 | tf_op jit(solution)/shard_map/while/body/eval_jaxpr/sub | solution.py:42
  308.7 5.9 %fusion.45 = bf16[16,6,32,128]{3,2,1,0:T(8,128)(2,1)S(1)} fusion(bf16[16,256,6,32]{1,3,2,0:T(8,128)(2,1)S(1)} %bitcast.65, f32[16,6,128,256]{3,2,1,0:T(8,128)} %get-tuple-element.113, f32[16,6,128]{2,1,0:T(8,128)S(1)} %get-tuple-element.114), kind=kOutput, calls=%fused_computation.15.clone.1 | convolution fusion | flops 208011264 | bytes 14991360 | tf_op jit(solution)/shard_map/while/body/eval_jaxpr/ghqk,gkhd->gqhd/dot_general | solution.py:44
  318.6 1.6 constant_dynamic-slice_fusion.7
  321.2 1.7 constant_dynamic-slice_fusion.8
  324.8 10.3 %fusion.44 = (f32[16,6,128]{2,1,0:T(8,128)S(1)}, f32[16,6,128,256]{3,2,1,0:T(8,128)}) fusion(pred[16,256]{1,0:T(8,128)(4,1)S(1)} %concatenate.11, bf16[16,128,6,32]{1,3,2,0:T(8,128)(2,1)} %bitcast.69, bf16[16,256,6,32]{1,3,2,0:T(8,128)(2,1)} %bitcast.66), kind=kOutput, calls=%fused_computation.47.clone.1 | convolution fusion | flops 213909760 | bytes 14995456 | tf_op jit(solution)/shard_map/while/body/eval_jaxpr/sub | solution.py:42
  335.1 5.9 %fusion.45 = bf16[16,6,32,128]{3,2,1,0:T(8,128)(2,1)S(1)} fusion(bf16[16,256,6,32]{1,3,2,0:T(8,128)(2,1)S(1)} %bitcast.65, f32[16,6,128,256]{3,2,1,0:T(8,128)} %get-tuple-element.113, f32[16,6,128]{2,1,0:T(8,128)S(1)} %get-tuple-element.114), kind=kOutput, calls=%fused_computation.15.clone.1 | convolution fusion | flops 208011264 | bytes 14991360 | tf_op jit(solution)/shard_map/while/body/eval_jaxpr/ghqk,gkhd->gqhd/dot_general | solution.py:44
  345.0 1.6 constant_dynamic-slice_fusion.7
  347.6 1.7 constant_dynamic-slice_fusion.8
  351.3 10.3 %fusion.44 = (f32[16,6,128]{2,1,0:T(8,128)S(1)}, f32[16,6,128,256]{3,2,1,0:T(8,128)}) fusion(pred[16,256]{1,0:T(8,128)(4,1)S(1)} %concatenate.11, bf16[16,128,6,32]{1,3,2,0:T(8,128)(2,1)} %bitcast.69, bf16[16,256,6,32]{1,3,2,0:T(8,128)(2,1)} %bitcast.66), kind=kOutput, calls=%fused_computation.47.clone.1 | convolution fusion | flops 213909760 | bytes 14995456 | tf_op jit(solution)/shard_map/while/body/eval_jaxpr/sub | solution.py:42
  361.6 5.9 %fusion.45 = bf16[16,6,32,128]{3,2,1,0:T(8,128)(2,1)S(1)} fusion(bf16[16,256,6,32]{1,3,2,0:T(8,128)(2,1)S(1)} %bitcast.65, f32[16,6,128,256]{3,2,1,0:T(8,128)} %get-tuple-element.113, f32[16,6,128]{2,1,0:T(8,128)S(1)} %get-tuple-element.114), kind=kOutput, calls=%fused_computation.15.clone.1 | convolution fusion | flops 208011264 | bytes 14991360 | tf_op jit(solution)/shard_map/while/body/eval_jaxpr/ghqk,gkhd->gqhd/dot_general | solution.py:44
  368.9 10.1 %convolution_convert_fusion.1 = bf16[16384,192]{0,1:T(8,128)(2,1)} fusion(bf16[192,192]{1,0:T(8,128)(2,1)S(1)} %copy-done.4, bf16[24,8,128,128]{3,2,1,0:T(8,128)(2,1)} %bitcast.72), kind=kOutput, calls=%fused_computation.27 | convolution fusion | flops 1211105280 | bytes 12656640 | tf_op jit(solution)/shard_map/dot_general | solution.py:75
  (102 shorter events, 56.5 us)
Async XLA Ops:
  0.0 6.4 %copy-start = (bf16[192,576]{1,0:T(8,128)(2,1)S(1)}, bf16[192,576]{1,0:T(8,128)(2,1)}, u32[]{:S(2)}) copy-start(bf16[192,576]{1,0:T(8,128)(2,1)} %param.10) | copy-start | bytes 663556
  0.0 4.6 %copy-start.3 = (bf16[16384,192]{0,1:T(8,128)(2,1)S(1)}, bf16[16384,192]{0,1:T(8,128)(2,1)}, u32[]{:S(2)}) copy-start(bf16[16384,192]{0,1:T(8,128)(2,1)} %param.8) | copy-start | bytes 18874372
  0.0 6.4 %copy-start.7 = (f32[192]{0:T(256)S(1)}, f32[192]{0:T(256)}, u32[]{:S(2)}) copy-start(f32[192]{0:T(256)} %param.9) | copy-start | bytes 2308
  17.2 41.6 %collective-permute-start = (bf16[1024,384]{0,1:T(8,128)(2,1)S(1)}, bf16[1024,384]{0,1:T(8,128)(2,1)S(1)}, u32[]{:S(2)}, u32[]{:S(2)}) collective-permute-start(bf16[1024,384]{0,1:T(8,128)(2,1)S(1)} %get-tuple-element.66), channel_id=1, source_target_pairs={{0,1},{1,2},{2,3},{3,4},{4,5},{5,6},{6,7},{7,8},{8,9},{9,10},{10,1... | collective-permute-start | bytes 2359304 | tf_op jit(solution)/shard_map/ppermute | solution.py:18
  21.8 37.1 %collective-permute-start.1 = (bf16[1024,384]{0,1:T(8,128)(2,1)S(1)}, bf16[1024,384]{0,1:T(8,128)(2,1)S(1)}, u32[]{:S(2)}, u32[]{:S(2)}) collective-permute-start(bf16[1024,384]{0,1:T(8,128)(2,1)S(1)} %get-tuple-element.67), channel_id=1, source_target_pairs={{1,0},{2,1},{3,2},{4,3},{5,4},{6,5},{7,6},{8,7},{9,8},{10,9},{11,1... | collective-permute-start | bytes 2359304 | tf_op jit(solution)/shard_map/ppermute | solution.py:21
  38.1 6.1 %copy-start.6 = (s32[128]{0:T(128)S(1)}, s32[128]{0:T(128)}, u32[]{:S(2)}) copy-start(s32[128]{0:T(128)} %param.12) | copy-start | bytes 1540
  44.3 7.7 %copy-start.2 = (bf16[48,8,128,128]{3,1,2,0:T(8,128)(2,1)S(1)}, bf16[48,8,128,128]{3,1,2,0:T(8,128)(2,1)}, u32[]{:S(2)}) copy-start(bf16[48,8,128,128]{3,1,2,0:T(8,128)(2,1)} %get-tuple-element.69) | copy-start | bytes 37748740
  51.9 7.0 %slice-start = ((s8[12582912]{0:T(1024)(128)(4,1)}), s8[4194304]{0:T(1024)(128)(4,1)S(1)}, s32[]{:S(2)}) async-start(s8[12582912]{0:T(1024)(128)(4,1)} %bitcast.63), calls=%async_computation | async-start | bytes 8388608
  52.0 6.7 %copy-start.5 = (s32[128,128]{1,0:T(8,128)S(1)}, s32[128,128]{1,0:T(8,128)}, u32[]{:S(2)}) copy-start(s32[128,128]{1,0:T(8,128)} %param.13) | copy-start | bytes 196612
  52.0 7.3 %slice-start.1 = ((s8[12582912]{0:T(1024)(128)(4,1)}), s8[4194304]{0:T(1024)(128)(4,1)S(1)}, s32[]{:S(2)}) async-start(s8[12582912]{0:T(1024)(128)(4,1)} %bitcast.63), calls=%async_computation.1 | async-start | bytes 8388608
  52.1 8.8 %slice-start.2 = ((s8[12582912]{0:T(1024)(128)(4,1)}), s8[4194304]{0:T(1024)(128)(4,1)S(1)}, s32[]{:S(2)}) async-start(s8[12582912]{0:T(1024)(128)(4,1)} %bitcast.63), calls=%async_computation.2 | async-start | bytes 8388608
  157.5 211.4 %copy-start.4 = (bf16[192,192]{1,0:T(8,128)(2,1)S(1)}, bf16[192,192]{1,0:T(8,128)(2,1)}, u32[]{:S(2)}) copy-start(bf16[192,192]{1,0:T(8,128)(2,1)} %param.11) | copy-start | bytes 221188
  368.9 10.1 %copy-start.1 = (bf16[192,576]{1,0:T(8,128)(2,1)S(1)}, bf16[192,576]{1,0:T(8,128)(2,1)}, u32[]{:S(2)}) copy-start(bf16[192,576]{1,0:T(8,128)(2,1)} %param.10) | copy-start | bytes 663556
where the time goes:
time: 381 us; the launch traced here: 379 us
  local copies, waits for them, and re-layouts  197 us (52%)
  matrix products  149 us (39%)
  other arithmetic  25.9 us (7%)
  starting transfers between devices  6.46 us (2%)
    sub x8, matrix products, attend_windows(): expo = jnp.exp(scores - top)  82.4 us
    gather x1, local copies, waits for them, and re-layouts, shards(): far_rows = jnp.take(extended, local_index, axis=0, mode='clip')  70.7 us
    dynamic_slice x48, local copies, waits for them, and re-layouts, shards(): mixed = lax.map(one_block, (q4, kv4, far4, live)).reshape(rows, width)  57 us
    dot_general x8, matrix products, attend_windows(): jnp.einsum('ghqk,gkhd->gqhd', prob, values, preferred_element_type=jnp.fl...  47.1 us
    unnamed x25, local copies, waits for them, and re-layouts  23.2 us
    concatenate x1, local copies, waits for them, and re-layouts, extended_2(): block = jnp.concatenate([low, block, high], axis=dim)  18.5 us
    slice x1, local copies, waits for them, and re-layouts, shards(): keyvals = qkv[:, width:]  14.4 us
    concatenate x8, other arithmetic, attend_windows(): allkv = jnp.concatenate([dense_kv, far_kv], axis=1)  12.1 us
  transfers between devices with their start and end apart: 2, of which 0 were waited for; matrix products, arithmetic and copies ran while one was open for 9% of the time, Pallas kernels for 0%

commit v1 on v0

v1 whole, which is shorter than its diff:
```python
import functools
import math

import jax
import jax.numpy as jnp
from jax import lax
from jax.experimental import pallas as pl
from jax.experimental.pallas import tpu as pltpu
from jax.sharding import PartitionSpec as P

HEADS = 6
WIN = 128
REACH = 1024
LANES = 128
PARTS = 4
BIAS = 64
DEAD = -1e30


def project(x, row, live, gain, wq, wkv, store, queries=None, column=None):
    xf = x.astype(jnp.float32)
    width, size = xf.shape
    mean = jnp.sum(xf, axis=0, keepdims=True) / width
    centred = xf - mean
    var = jnp.sum(centred * centred, axis=0, keepdims=True) / width
    scale = 1.0 / jnp.sqrt(var + 1e-05)
    normed = (centred * scale * gain).astype(jnp.bfloat16)
    if queries is not None:
        q = jnp.dot(wq, normed, preferred_element_type=jnp.float32)
        queries[:, pl.ds(column, size)] = q.astype(jnp.bfloat16)
    kv = lax.dot_general(
        normed, wkv, (((0,), (0,)), ((), ())), preferred_element_type=jnp.float32
    )
    kv = kv.astype(jnp.bfloat16).astype(jnp.float32)
    for part in range(PARTS):
        piece = kv[:, part * LANES : (part + 1) * LANES]
        if part == 1 and live is not None:
            lane = lax.broadcasted_iota(jnp.int32, (WIN, LANES), 1)
            slot = lax.broadcasted_iota(jnp.int32, (WIN, LANES), 0)
            bias = [
                jnp.where((lane == BIAS) & (slot >= count), DEAD, 0.0) for count in live
            ]
            piece = piece + jnp.concatenate(bias, axis=0)
        store[pl.ds(row * PARTS + part, size, stride=PARTS), :] = piece


def prepare(window, far_ref, store, far_rows, spread, queries, width):
    head_dim = width // HEADS
    for j in range(WIN):
        at = far_ref[window, j]
        far_rows[pl.ds(j * PARTS, PARTS), :] = store[
            pl.ds(pl.multiple_of(at * PARTS, PARTS), PARTS), :
        ]
    own = (window * WIN + REACH) * PARTS
    pieces = []
    for part in range(PARTS):
        dense = store[pl.ds(own + part, WIN, stride=PARTS), :]
        far = far_rows[pl.ds(part, WIN, stride=PARTS), :]
        pieces.append(jnp.concatenate([dense, far], axis=0))
    keys = jnp.concatenate([pieces[0], pieces[1]], axis=1).astype(jnp.bfloat16)
    values = jnp.concatenate(
        [pieces[2].T.astype(jnp.bfloat16), pieces[3].T[: LANES // 2].astype(jnp.bfloat16)],
        axis=0,
    )
    q = queries[:, pl.ds(pl.multiple_of(window * WIN, WIN), WIN)]
    for h in range(HEADS):
        spread[pl.ds(h * head_dim, head_dim), pl.ds(h * WIN, WIN)] = q[
            h * head_dim : (h + 1) * head_dim
        ]
    return keys, values


HP = 2


def scores(keys, spread, item):
    return jnp.dot(
        keys,
        spread[:, pl.ds(item * HP * WIN, HP * WIN)],
        preferred_element_type=jnp.float32,
    )


def soft(s2, head_dim):
    factor = math.log2(math.e) / math.sqrt(head_dim)
    top = jnp.max(s2, axis=0, keepdims=True)
    expo = jnp.exp2((s2 - top) * factor)
    inverse = 1.0 / jnp.sum(expo, axis=0, keepdims=True)
    return (expo * inverse).astype(jnp.bfloat16)


def mix(values, prob, item, head_dim):
    out = jnp.dot(
        values[item * HP * head_dim : (item + 1) * HP * head_dim],
        prob,
        preferred_element_type=jnp.float32,
    )
    return [out[i * head_dim : (i + 1) * head_dim, i * WIN : (i + 1) * WIN] for i in range(HP)]


def attend_group(first, group, far_ref, store, far_rows, spread, queries, w_out, width, out):
    head_dim = width // HEADS
    per = HEADS // HP
    items = [(i, p) for i in range(group) for p in range(per)]
    ready, pending, probs, mixed = {}, {}, {}, {}

    def get_ready(n):
        i, p = items[n]
        if p == 0:
            ready[i] = prepare(first + i, far_ref, store, far_rows.at[i], spread.at[i], queries, width)

    def score(n):
        i, p = items[n]
        pending[n] = scores(ready[i][0], spread.at[i], p)

    def blend(n):
        i, p = items[n]
        mixed.setdefault(i, []).extend(mix(ready[i][1], probs.pop(n), p, head_dim))

    def finish(n):
        i, p = items[n]
        if p == per - 1:
            m = jnp.concatenate(mixed.pop(i), axis=0).astype(jnp.bfloat16)
            out[:, i * WIN : (i + 1) * WIN] = jnp.dot(
                w_out, m, preferred_element_type=jnp.float32).astype(jnp.bfloat16)

    def softmax(n):
        probs[n] = soft(pending.pop(n), head_dim)

    stages = ((get_ready, 0), (score, PREP), (softmax, PREP + AHEAD), (blend, PREP + AHEAD + BEHIND), (finish, PREP + AHEAD + BEHIND + TAIL))
    for n in range(len(items) + stages[-1][1]):
        for run, late in stages:
            if 0 <= n - late < len(items):
                run(n - late)


AHEAD, BEHIND, PREP, TAIL = 3,2,3,1


def body(
    steps, block, group, far_ref, live_ref, low, own, high, gain, wq, wkv, w_out, out,
    store, queries, far_rows, spread,
):
    low_steps, own_steps, high_steps = steps
    width = own.shape[0]
    step = pl.program_id(0)
    per = block // WIN

    @pl.when(step == 0)
    def _():
        for slot in range(group):
            spread[slot, :, :] = jnp.zeros(spread.shape[1:], spread.dtype)
            spread[slot, LANES + BIAS : LANES + BIAS + 16, :] = jnp.where(
                lax.broadcasted_iota(jnp.int32, (16, spread.shape[2]), 0) == 0, 1.0, 0.0
            ).astype(spread.dtype)

    row = pl.multiple_of(step * block, block)

    @pl.when(step < low_steps)
    def _():
        project(low[...], row, None, gain[...], wq[...], wkv[...], store)

    @pl.when((step >= low_steps) & (step < low_steps + own_steps))
    def _():
        first = (step - low_steps) * per
        live = [live_ref[first + i] for i in range(per)]
        column = pl.multiple_of((step - low_steps) * block, block)
        project(
            own[...], row, live, gain[...], wq[...], wkv[...], store, queries, column
        )

    @pl.when((step >= low_steps + own_steps) & (step < sum(steps)))
    def _():
        project(high[...], row, None, gain[...], wq[...], wkv[...], store)

    @pl.when(step >= sum(steps))
    def _():
        first = (step - sum(steps)) * group
        attend_group(first, group, far_ref, store, far_rows, spread, queries, w_out[...], width, out)


def local(points, low, high, gain, wq, wkv, w_out, counts, far, block=512, group=8):
    width, rows = points.shape
    reach = low.shape[1]
    windows = rows // WIN
    steps = (reach // block, rows // block, reach // block)
    before = sum(steps)
    total = rows + 2 * reach
    whole = lambda shape: pl.BlockSpec(shape, lambda t, *_: (0, 0))
    last = lambda t, start, count: (0, jnp.clip(t - start, 0, count - 1))
    return pl.pallas_call(
        functools.partial(body, steps, block, group),
        out_shape=jax.ShapeDtypeStruct((width, rows), jnp.bfloat16),
        grid_spec=pltpu.PrefetchScalarGridSpec(
            num_scalar_prefetch=2,
            grid=(before + windows // group,),
            in_specs=[
                pl.BlockSpec((width, block), lambda t, *_: last(t, 0, steps[0])),
                pl.BlockSpec((width, block), lambda t, *_: last(t, steps[0], steps[1])),
                pl.BlockSpec(
                    (width, block), lambda t, *_: last(t, steps[0] + steps[1], steps[2])
                ),
                whole(gain.shape),
                whole(wq.shape),
                whole(wkv.shape),
                whole(w_out.shape),
            ],
            out_specs=pl.BlockSpec(
                (width, group * WIN), lambda t, *_: (0, jnp.maximum(t - before, 0))
            ),
            scratch_shapes=[
                pltpu.VMEM((total * PARTS, LANES), jnp.float32),
                pltpu.VMEM((width, rows), jnp.bfloat16),
                pltpu.VMEM((group, WIN * PARTS, LANES), jnp.float32),
                pltpu.VMEM((group, 2 * LANES, HEADS * WIN), jnp.bfloat16),
            ],
        ),
        compiler_params=pltpu.CompilerParams(vmem_limit_bytes=60 << 20),
    )(far, counts, low, points, high, gain, wq, wkv, w_out)


def weights(w_qkv, w_out, width):
    head_dim = width // HEADS
    cut = LANES // head_dim * head_dim
    wq = w_qkv[:, :width].T
    k, v = w_qkv[:, width : 2 * width], w_qkv[:, 2 * width :]
    pad = jnp.zeros((width, 2 * LANES - width), w_qkv.dtype)
    wkv = jnp.concatenate([k[:, :cut], k[:, cut:], pad, v[:, :cut], v[:, cut:], pad], axis=1)
    return wq, wkv, w_out.T


def shards(points, gain, w_qkv, w_out, counts, far_index):
    rows, width = points.shape
    x = points.T
    count = lax.axis_size("gx")
    forward = [(i, i + 1) for i in range(count - 1)]
    backward = [(i + 1, i) for i in range(count - 1)]
    low = lax.ppermute(x[:, rows - REACH :], "gx", forward)
    high = lax.ppermute(x[:, :REACH], "gx", backward)
    windows = rows // WIN
    far = far_index + (jnp.arange(windows, dtype=jnp.int32) * WIN)[:, None]
    wq, wkv, wo = weights(w_qkv, w_out, width)
    out = local(x, low, high, gain[:, None], wq, wkv, wo, counts, far)
    return out.T


def solution(mesh):
    return jax.shard_map(
        shards,
        mesh=mesh,
        in_specs=(
            P(("tile", "gx"), None),
            P(),
            P(),
            P(),
            P(("tile", "gx")),
            P(("tile", "gx"), None),
        ),
        out_specs=P(("tile", "gx"), None),
        check_vma=False,
    )
```

time: 381 us -> 103 us (0.27)
  local copies, waits for them, and re-layouts: 197 us -> 6.82 us
  matrix products: 149 us -> 0 us
  Pallas kernels: 0 us -> 85.4 us
  other arithmetic: 25.9 us -> 2.33 us
    pallas_call x0 -> x1, Pallas kernels: none -> 85.4 us  [local(): pl.pallas_call(functools.partial(body, steps, block, group), out_shape=ja...]
    sub x8 -> x0, matrix products: 82.4 us -> none  [attend_windows(): expo = jnp.exp(scores - top)]
    gather x1 -> x0, local copies, waits for them, and re-layouts: 70.7 us -> none  [shards(): far_rows = jnp.take(extended, local_index, axis=0, mode='clip')]
    dot_general x10 -> x0, matrix products: 66.4 us -> none  [the longest x8 47.1 us: attend_windows(): jnp.einsum('ghqk,gkhd->gqhd', prob, values, preferred_element_type=jnp.fl...]
    dynamic_slice x48 -> x0, local copies, waits for them, and re-layouts: 57 us -> none  [shards(): mixed = lax.map(one_block, (q4, kv4, far4, live)).reshape(rows, width)]
    unnamed x25 -> x6, local copies, waits for them, and re-layouts: 23.2 us -> 3.1 us
    concatenate x9 -> x1, other arithmetic: 19.5 us -> 0.79 us  [weights(): jnp.concatenate([k[:, :cut], k[:, cut:], pad, v[:, :cut], v[:, cut:], pad...]
    concatenate x9 -> x0, local copies, waits for them, and re-layouts: 18.6 us -> none  [the longest x1 18.5 us: extended_2(): block = jnp.concatenate([low, block, high], axis=dim)]
  transfers between devices with their start and end apart: 2 -> 2, of which waited for: 0 -> 1; matrix products, arithmetic and copies ran while one was open for 9% -> 7% of each run, Pallas kernels for 0% -> 0%
where the time goes in v1:
time: 103 us; the launch traced here: 102 us
  Pallas kernels  85.4 us (83%)
  local copies, waits for them, and re-layouts  6.82 us (7%)
  starting transfers between devices  6.46 us (6%)
  other arithmetic  2.33 us (2%)
    pallas_call x1, Pallas kernels, local(): pl.pallas_call(functools.partial(body, steps, block, group), out_shape=ja...  85.4 us
    ppermute x1, starting transfers between devices, shards(): low = lax.ppermute(x[:, rows - REACH:], 'gx', forward)  4.49 us
    unnamed x6, local copies, waits for them, and re-layouts  3.1 us
  transfers between devices with their start and end apart: 2, of which 1 were waited for; matrix products, arithmetic and copies ran while one was open for 7% of the time, Pallas kernels for 0%

profile of v1, /device:TPU:1, one launch (start us, length us, event | category | flops | bytes accessed | tf_op | source)
XLA Modules:
  0.0 101.6 jit_solution(13198337758288862034)
XLA Ops:
  0.0 1.2 %fusion = (bf16[192,1024]{1,0:T(8,128)(2,1)S(1)}, bf16[192,1024]{1,0:T(8,128)(2,1)S(1)}) fusion(bf16[192,16384]{1,0:T(8,128)(2,1)} %bitcast.5), kind=kLoop, calls=%fused_computation.3 | loop fusion | bytes 1572864 | tf_op jit(solution)/shard_map/slice | solution.py:239
  1.2 2.0 %collective-permute-start.1 = (bf16[192,1024]{1,0:T(8,128)(2,1)S(1)}, bf16[192,1024]{1,0:T(8,128)(2,1)S(1)}, u32[]{:S(2)}, u32[]{:S(2)}) collective-permute-start(bf16[192,1024]{1,0:T(8,128)(2,1)S(1)} %get-tuple-element.5), channel_id=1, source_target_pairs={{1,0},{2,1},{3,2},{4,3},{5,4},{6,5},{7,6},{8,7},{9,8},{10,9},{11,1... | collective-permute-start | bytes 1179656 | tf_op jit(solution)/shard_map/ppermute | solution.py:239
  3.1 4.5 %collective-permute-start = (bf16[192,1024]{1,0:T(8,128)(2,1)S(1)}, bf16[192,1024]{1,0:T(8,128)(2,1)S(1)}, u32[]{:S(2)}, u32[]{:S(2)}) collective-permute-start(bf16[192,1024]{1,0:T(8,128)(2,1)S(1)} %get-tuple-element.6), channel_id=1, source_target_pairs={{0,1},{1,2},{2,3},{3,4},{4,5},{5,6},{6,7},{7,8},{8,9},{9,10},{10,1... | collective-permute-start | bytes 1179656 | tf_op jit(solution)/shard_map/ppermute | solution.py:238
  7.6 1.1 %fusion.1 = (bf16[192,192]{1,0:T(8,128)(2,1)S(1)}, bf16[192,192]{1,0:T(8,128)(2,1)S(1)}, bf16[192,192]{1,0:T(8,128)(2,1)S(1)}) fusion(bf16[192,576]{1,0:T(8,128)(2,1)} %param.8), kind=kLoop, calls=%fused_computation.4 | loop fusion | bytes 442368 | tf_op jit(solution)/shard_map/slice | solution.py:228
  8.8 1.4 %copy.11.gain = f32[192,1]{1,0:T(8,128)} copy(f32[192,1]{0,1:T(1,128)} %bitcast.9) | data formatting | bytes 1536 | tf_op jit(solution)/shard_map/broadcast_in_dim | solution.py:243
  10.2 1.6 %copy.10 = bf16[192,192]{0,1:T(8,128)(2,1)} copy(bf16[192,192]{1,0:T(8,128)(2,1)} %param.9) | data formatting | bytes 147456 | tf_op args[3]
  11.8 0.7 copy.12
  12.6 0.8 pad_maximum_fusion.wkv
  13.4 1.5 %broadcast_add_fusion.far_ref = s32[128,128]{1,0:T(8,128)} fusion(s32[128,128]{1,0:T(8,128)} %param.11, s32[128]{0:T(128)S(1)} %iota_multiply_fusion), kind=kLoop, calls=%fused_computation.1 | loop fusion | flops 16384 | bytes 131584 | tf_op jit(solution)/shard_map/add | solution.py:241
  14.9 0.0 collective-permute-done.1.high
  14.9 0.0 copy-start
  14.9 0.6 collective-permute-done.low
  15.5 0.0 copy-start.1
  15.5 0.1 copy-done
  15.7 0.6 copy-done.1
  16.3 85.4 %shard_map.64 = bf16[192,16384]{1,0:T(8,128)(2,1)} custom-call(s32[128,128]{1,0:T(8,128)} %broadcast_add_fusion.far_ref, s32[128]{0:T(128)} %live_ref.1, bf16[192,1024]{1,0:T(8,128)(2,1)} %copy-done.1, bf16[192,16384]{1,0:T(8,128)(2,1)} %bitcast.6, bf16[192,1024]{1,0:T(8,128)(2,1)} %copy-done, f32[192,1]{1,0:T(8,128)} %copy.11.gain, ...), custom_call_target="tpu_custom_call" | custom-call | tf_op jit(solution)/shard_map/pallas_call | solution.py:191
  (2 shorter events, 0.0 us)
Async XLA Ops:
  1.2 13.7 %collective-permute-start.1 = (bf16[192,1024]{1,0:T(8,128)(2,1)S(1)}, bf16[192,1024]{1,0:T(8,128)(2,1)S(1)}, u32[]{:S(2)}, u32[]{:S(2)}) collective-permute-start(bf16[192,1024]{1,0:T(8,128)(2,1)S(1)} %get-tuple-element.5), channel_id=1, source_target_pairs={{1,0},{2,1},{3,2},{4,3},{5,4},{6,5},{7,6},{8,7},{9,8},{10,9},{11,1... | collective-permute-start | bytes 1179656 | tf_op jit(solution)/shard_map/ppermute | solution.py:239
  3.1 12.4 %collective-permute-start = (bf16[192,1024]{1,0:T(8,128)(2,1)S(1)}, bf16[192,1024]{1,0:T(8,128)(2,1)S(1)}, u32[]{:S(2)}, u32[]{:S(2)}) collective-permute-start(bf16[192,1024]{1,0:T(8,128)(2,1)S(1)} %get-tuple-element.6), channel_id=1, source_target_pairs={{0,1},{1,2},{2,3},{3,4},{4,5},{5,6},{6,7},{7,8},{8,9},{9,10},{10,1... | collective-permute-start | bytes 1179656 | tf_op jit(solution)/shard_map/ppermute | solution.py:238
  14.9 0.8 copy-start
  15.5 0.7 copy-start.1

commit v2 on v0

v2 whole, which is shorter than its diff:
```python
import functools
import math

import jax
import jax.numpy as jnp
from jax import lax
from jax.experimental import pallas as pl
from jax.experimental.pallas import tpu as pltpu
from jax.sharding import PartitionSpec as P

HEADS = 6
WIN = 128
REACH = 1024
LANES = 128
PARTS = 4
PAD = 2 * PARTS
BIAS = 64
DEAD = -1e30
BLOCK = 1024
SUB = 256
GROUP = 16
SLOTS = 4
PAIR = 2
EARLY, PREP, AHEAD, BEHIND, TAIL = 4, 3, 3, 3, 2


def pipelined(count, stages):
    for n in range(count + max(lag for _, lag in stages)):
        for run, lag in stages:
            if 0 <= n - lag < count:
                run(n - lag)


def project(xq, column, gain, wq, wkv, store, live=None, queries=True):
    width = xq.shape[0]
    norms, dots = {}, {}

    def norm(n):
        xf = xq[:, pl.ds(column + n * SUB, SUB)].astype(jnp.float32)
        mean = jnp.sum(xf, axis=0, keepdims=True) / width
        centred = xf - mean
        var = jnp.sum(centred * centred, axis=0, keepdims=True) / width
        scale = 1.0 / jnp.sqrt(var + 1e-05)
        full = jnp.concatenate([gain[...]] * (SUB // LANES), axis=1)
        norms[n] = (centred * scale * full).astype(jnp.bfloat16)

    def dot(n):
        normed = norms.pop(n)
        q = None
        if queries:
            q = jnp.dot(wq[...], normed, preferred_element_type=jnp.float32)
        kv = lax.dot_general(
            normed, wkv[...], (((0,), (0,)), ((), ())), preferred_element_type=jnp.float32
        )
        dots[n] = q, kv

    def keep(n):
        q, kv = dots.pop(n)
        if queries:
            xq[:, pl.ds(column + n * SUB, SUB)] = q.astype(jnp.bfloat16)
        kv = kv.astype(jnp.bfloat16).astype(jnp.float32)
        for part in range(PARTS):
            piece = kv[:, part * LANES : (part + 1) * LANES]
            if part == 1 and live is not None:
                lane = lax.broadcasted_iota(jnp.int32, (WIN, LANES), 1)
                slot = lax.broadcasted_iota(jnp.int32, (WIN, LANES), 0)
                bias = [
                    jnp.where((lane == BIAS) & (slot >= live(n * SUB // WIN + i)), DEAD, 0.0)
                    for i in range(SUB // WIN)
                ]
                piece = piece + jnp.concatenate(bias, axis=0)
            store[pl.ds(PAD + (column + n * SUB) * PARTS + part, SUB, stride=PARTS), :] = piece

    pipelined(BLOCK // SUB, ((norm, 0), (dot, 1), (keep, 2)))


def attend(column, window, far_ref, xq, w_out, store, far_rows, spread):
    width = xq.shape[0]
    head_dim = width // HEADS
    factor = math.log2(math.e) / math.sqrt(head_dim)
    per = HEADS // PAIR
    ready, pending, probs, mixed = {}, {}, {}, {}

    def gather(n):
        i, p = divmod(n, per)
        base = (pl.multiple_of(column + i * WIN, WIN) - REACH) * PARTS
        rows = far_rows.at[i % SLOTS]
        upper = lax.broadcasted_iota(jnp.int32, (2 * PARTS, LANES), 0) >= PARTS
        for j in range(p * WIN // per // 2 * 2, (p + 1) * WIN // per // 2 * 2, 2):
            one, two = [
                store[pl.ds(pl.multiple_of(at, PARTS), 2 * PARTS), :]
                for at in (
                    base + PAD + far_ref[window + i, j] * PARTS,
                    base + PAD - PARTS + far_ref[window + i, j + 1] * PARTS,
                )
            ]
            rows[pl.ds(j * PARTS, 2 * PARTS), :] = jnp.where(upper, two, one)

    def prepare(n):
        if n % per:
            return
        i = n // per
        own = pl.multiple_of(column + i * WIN, WIN)
        rows = far_rows.at[i % SLOTS]
        pieces = []
        for part in range(PARTS):
            dense = store[pl.ds(PAD + own * PARTS + part, WIN, stride=PARTS), :]
            far = rows[pl.ds(part, WIN, stride=PARTS), :]
            pieces.append(jnp.concatenate([dense, far], axis=0))
        keys = jnp.concatenate(pieces[:2], axis=1).astype(jnp.bfloat16)
        values = [pieces[2].T, pieces[3].T[: width - LANES]]
        values = jnp.concatenate(values, axis=0).astype(jnp.bfloat16)
        q = xq[:, pl.ds(own, WIN)]
        for h in range(HEADS):
            head = slice(h * head_dim, (h + 1) * head_dim)
            spread[i % SLOTS, head, h * WIN : (h + 1) * WIN] = q[head]
        ready[i] = keys, values

    def score(n):
        i, p = divmod(n, per)
        pending[n] = jnp.dot(
            ready[i][0],
            spread[i % SLOTS, :, p * PAIR * WIN : (p + 1) * PAIR * WIN],
            preferred_element_type=jnp.float32,
        )

    def softmax(n):
        s2 = pending.pop(n)
        halves = []
        for h in range(PAIR):
            s = s2[:, h * WIN : (h + 1) * WIN]
            top = jnp.max(s, axis=0, keepdims=True)
            expo = jnp.exp2((s - top) * factor)
            inverse = 1.0 / jnp.sum(expo, axis=0, keepdims=True)
            halves.append((expo * inverse).astype(jnp.bfloat16))
        probs[n] = jnp.concatenate(halves, axis=1)

    def blend(n):
        i, p = divmod(n, per)
        out = jnp.dot(
            ready[i][1][p * PAIR * head_dim : (p + 1) * PAIR * head_dim],
            probs.pop(n),
            preferred_element_type=jnp.float32,
        )
        for h in range(PAIR):
            piece = out[h * head_dim : (h + 1) * head_dim, h * WIN : (h + 1) * WIN]
            mixed.setdefault(i, []).append(piece)

    def finish(n):
        i, p = divmod(n, per)
        if p < per - 1:
            return
        m = jnp.concatenate(mixed.pop(i), axis=0).astype(jnp.bfloat16)
        out = jnp.dot(w_out[...], m, preferred_element_type=jnp.float32)
        xq[:, pl.ds(column + i * WIN, WIN)] = out.astype(jnp.bfloat16)

    lags = [EARLY, PREP, AHEAD, BEHIND, TAIL]
    lags = [sum(lags[:i]) for i in range(6)]
    pipelined(GROUP * per, tuple(zip((gather, prepare, score, softmax, blend, finish), lags)))


def arrange(gain, w_qkv, w_out, full_gain, wq, wkv, wo):
    width = w_qkv.shape[0]
    f32 = jnp.float32
    full_gain[...] = jnp.broadcast_to(gain[...], (LANES, width)).T
    w = w_qkv[...].astype(f32)
    wq[...] = w[:, :width].T.astype(wq.dtype)
    wo[...] = w_out[...].astype(f32).T.astype(wo.dtype)
    pad = jnp.zeros((width, 2 * LANES - width), f32)
    parts = []
    for first in (width, 2 * width):
        parts += [w[:, first : first + width], pad]
    wkv[...] = jnp.concatenate(parts, axis=1).astype(wkv.dtype)


def body(
    far_ref, live_ref, x, low, high, gain, w_qkv, w_out, out,
    store, xq, far_rows, spread, full_gain, wq, wkv, wo, got, sent,
):
    width, rows = x.shape
    reach = low.shape[1]
    halo, main = reach // BLOCK, rows // BLOCK

    def fetch(src, at, column, size, slot):
        return pltpu.make_async_copy(
            src.at[:, pl.ds(at, size)], xq.at[:, pl.ds(column, size)], got.at[slot]
        )

    copies = [fetch(x, i * BLOCK, reach + i * BLOCK, BLOCK, i) for i in range(main)]
    copies += [fetch(low, i * BLOCK, i * BLOCK, BLOCK, main + i) for i in range(halo)]
    copies += [
        fetch(high, i * BLOCK, reach + rows + i * BLOCK, BLOCK, main + halo + i)
        for i in range(halo)
    ]
    for copy in copies:
        copy.start()
    arrange(gain, w_qkv, w_out, full_gain, wq, wkv, wo)
    for slot in range(SLOTS):
        spread[slot, :, :] = jnp.zeros(spread.shape[1:], spread.dtype)
        ones = lax.broadcasted_iota(jnp.int32, (16, spread.shape[2]), 0) == 0
        spread[slot, LANES + BIAS : LANES + BIAS + 16, :] = jnp.where(ones, 1.0, 0.0).astype(
            spread.dtype
        )

    def own_block(i, _):
        column = pl.multiple_of(reach + i * BLOCK, BLOCK)
        fetch(x, pl.multiple_of(i * BLOCK, BLOCK), column, BLOCK, i).wait()
        live = lambda n: live_ref[i * (BLOCK // WIN) + n]
        project(xq, column, full_gain, wq, wkv, store, live)
        return 0

    lax.fori_loop(0, main, own_block, 0)
    for i in range(2 * halo):
        copies[main + i].wait()
        column = i * BLOCK if i < halo else rows + i * BLOCK
        project(xq, column, full_gain, wq, wkv, store, queries=False)

    span = GROUP * WIN

    def send(i):
        at = i * span if isinstance(i, int) else pl.multiple_of(i * span, span)
        return pltpu.make_async_copy(
            xq.at[:, pl.ds(reach + at, span)], out.at[:, pl.ds(at, span)], sent.at[i]
        )

    def own_group(i, _):
        column = pl.multiple_of(reach + i * span, span)
        attend(column, i * GROUP, far_ref, xq, wo, store, far_rows, spread)
        send(i).start()
        return 0

    lax.fori_loop(0, rows // span, own_group, 0)
    for i in range(rows // span):
        send(i).wait()


def local(x, low, high, gain, w_qkv, w_out, counts, far):
    width, rows = x.shape
    reach = low.shape[1]
    total = rows + 2 * reach
    blocks = total // BLOCK
    bf16 = jnp.bfloat16
    any_space = pl.BlockSpec(memory_space=pl.ANY)
    smem, vmem = pl.BlockSpec(memory_space=pltpu.SMEM), pl.BlockSpec(memory_space=pltpu.VMEM)
    return pl.pallas_call(
        body,
        out_shape=jax.ShapeDtypeStruct((width, rows), bf16),
        in_specs=[smem, smem, any_space, any_space, any_space, vmem, vmem, vmem],
        out_specs=any_space,
        scratch_shapes=[
            pltpu.VMEM((total * PARTS + 2 * PAD, LANES), jnp.float32),
            pltpu.VMEM((width, total), bf16),
            pltpu.VMEM((SLOTS, WIN * PARTS, LANES), jnp.float32),
            pltpu.VMEM((SLOTS, 2 * LANES, HEADS * WIN), bf16),
            pltpu.VMEM((width, LANES), jnp.float32),
            pltpu.VMEM((width, width), bf16),
            pltpu.VMEM((width, PARTS * LANES), bf16),
            pltpu.VMEM((width, width), bf16),
            pltpu.SemaphoreType.DMA((blocks,)),
            pltpu.SemaphoreType.DMA((rows // (GROUP * WIN),)),
        ],
        compiler_params=pltpu.CompilerParams(vmem_limit_bytes=60 << 20),
    )(far, counts, x, low, high, gain, w_qkv, w_out)


def shards(points, gain, w_qkv, w_out, counts, far_index):
    rows, width = points.shape
    x = points.T
    count = lax.axis_size("gx")
    forward = [(i, i + 1) for i in range(count - 1)]
    backward = [(i + 1, i) for i in range(count - 1)]
    low = lax.ppermute(x[:, rows - REACH :], "gx", forward)
    high = lax.ppermute(x[:, :REACH], "gx", backward)
    return local(x, low, high, gain[None, :], w_qkv, w_out, counts, far_index).T


def solution(mesh):
    return jax.shard_map(
        shards,
        mesh=mesh,
        in_specs=(
            P(("tile", "gx"), None),
            P(),
            P(),
            P(),
            P(("tile", "gx")),
            P(("tile", "gx"), None),
        ),
        out_specs=P(("tile", "gx"), None),
        check_vma=False,
    )
```

time: 381 us -> 84.5 us (0.22)
  local copies, waits for them, and re-layouts: 197 us -> 1.91 us
  matrix products: 149 us -> 0 us
  Pallas kernels: 0 us -> 68 us
  other arithmetic: 25.9 us -> 0 us
  waiting for transfers between devices: 0.01 us -> 7.89 us
    sub x8 -> x0, matrix products: 82.4 us -> none  [attend_windows(): expo = jnp.exp(scores - top)]
    gather x1 -> x0, local copies, waits for them, and re-layouts: 70.7 us -> none  [shards(): far_rows = jnp.take(extended, local_index, axis=0, mode='clip')]
    pallas_call x0 -> x1, Pallas kernels: none -> 68 us  [local(): pl.pallas_call(body, out_shape=jax.ShapeDtypeStruct((width, rows), bf16),...]
    dot_general x10 -> x0, matrix products: 66.4 us -> none  [the longest x8 47.1 us: attend_windows(): jnp.einsum('ghqk,gkhd->gqhd', prob, values, preferred_element_type=jnp.fl...]
    dynamic_slice x48 -> x0, local copies, waits for them, and re-layouts: 57 us -> none  [shards(): mixed = lax.map(one_block, (q4, kv4, far4, live)).reshape(rows, width)]
    unnamed x25 -> x4, local copies, waits for them, and re-layouts: 23.2 us -> 0.75 us
    concatenate x9 -> x0, other arithmetic: 19.5 us -> none  [the longest x8 12.1 us: attend_windows(): allkv = jnp.concatenate([dense_kv, far_kv], axis=1)]
    concatenate x9 -> x0, local copies, waits for them, and re-layouts: 18.6 us -> none  [the longest x1 18.5 us: extended_2(): block = jnp.concatenate([low, block, high], axis=dim)]
  transfers between devices with their start and end apart: 2 -> 2, of which waited for: 0 -> 2; matrix products, arithmetic and copies ran while one was open for 9% -> 0% of each run, Pallas kernels for 0% -> 0%
where the time goes in v2:
time: 84.5 us; the launch traced here: 84.3 us
  Pallas kernels  68 us (80%)
  waiting for transfers between devices  7.89 us (9%)
  starting transfers between devices  6.46 us (8%)
  local copies, waits for them, and re-layouts  1.91 us (2%)
    pallas_call x1, Pallas kernels, local(): pl.pallas_call(body, out_shape=jax.ShapeDtypeStruct((width, rows), bf16),...  68 us
    ppermute x1, starting transfers between devices, shards(): low = lax.ppermute(x[:, rows - REACH:], 'gx', forward)  4.49 us
    ppermute x1, waiting for transfers between devices, shards(): low = lax.ppermute(x[:, rows - REACH:], 'gx', forward)  4.38 us
    ppermute x1, waiting for transfers between devices, shards(): high = lax.ppermute(x[:, :REACH], 'gx', backward)  3.52 us
    ppermute x1, starting transfers between devices, shards(): high = lax.ppermute(x[:, :REACH], 'gx', backward)  1.97 us
  transfers between devices with their start and end apart: 2, of which 2 were waited for; matrix products, arithmetic and copies ran while one was open for 0% of the time, Pallas kernels for 0%

profile of v2, /device:TPU:1, one launch (start us, length us, event | category | flops | bytes accessed | tf_op | source)
XLA Modules:
  0.0 84.3 jit_solution(1992745225874628592)
XLA Ops:
  0.0 1.2 %fusion = (bf16[192,1024]{1,0:T(8,128)(2,1)S(1)}, bf16[192,1024]{1,0:T(8,128)(2,1)S(1)}) fusion(bf16[192,16384]{1,0:T(8,128)(2,1)} %bitcast.3), kind=kLoop, calls=%fused_computation | loop fusion | bytes 1572864 | tf_op jit(solution)/shard_map/slice | solution.py:273
  1.2 2.0 %collective-permute-start.1 = (bf16[192,1024]{1,0:T(8,128)(2,1)S(1)}, bf16[192,1024]{1,0:T(8,128)(2,1)S(1)}, u32[]{:S(2)}, u32[]{:S(2)}) collective-permute-start(bf16[192,1024]{1,0:T(8,128)(2,1)S(1)} %get-tuple-element.5), channel_id=1, source_target_pairs={{1,0},{2,1},{3,2},{4,3},{5,4},{6,5},{7,6},{8,7},{9,8},{10,9},{11,1... | collective-permute-start | bytes 1179656 | tf_op jit(solution)/shard_map/ppermute | solution.py:273
  3.1 4.5 %collective-permute-start = (bf16[192,1024]{1,0:T(8,128)(2,1)S(1)}, bf16[192,1024]{1,0:T(8,128)(2,1)S(1)}, u32[]{:S(2)}, u32[]{:S(2)}) collective-permute-start(bf16[192,1024]{1,0:T(8,128)(2,1)S(1)} %get-tuple-element.6), channel_id=1, source_target_pairs={{0,1},{1,2},{2,3},{3,4},{4,5},{5,6},{6,7},{7,8},{8,9},{9,10},{10,1... | collective-permute-start | bytes 1179656 | tf_op jit(solution)/shard_map/ppermute | solution.py:272
  7.6 3.5 %collective-permute-done.1.high = bf16[192,1024]{1,0:T(8,128)(2,1)S(1)} collective-permute-done((bf16[192,1024]{1,0:T(8,128)(2,1)S(1)}, bf16[192,1024]{1,0:T(8,128)(2,1)S(1)}, u32[]{:S(2)}, u32[]{:S(2)}) %collective-permute-start.1) | collective-permute-done | bytes 393248 | tf_op jit(solution)/shard_map/ppermute | solution.py:273
  11.2 0.0 copy-start
  11.2 4.4 %collective-permute-done.low = bf16[192,1024]{1,0:T(8,128)(2,1)S(1)} collective-permute-done((bf16[192,1024]{1,0:T(8,128)(2,1)S(1)}, bf16[192,1024]{1,0:T(8,128)(2,1)S(1)}, u32[]{:S(2)}, u32[]{:S(2)}) %collective-permute-start) | collective-permute-done | bytes 393248 | tf_op jit(solution)/shard_map/ppermute | solution.py:272
  15.5 0.0 copy-start.1
  15.5 0.0 copy-done
  15.5 0.7 copy-done.1
  16.3 68.0 %shard_map.64 = bf16[192,16384]{1,0:T(8,128)(2,1)} custom-call(s32[128,128]{1,0:T(8,128)} %far_ref.1, s32[128]{0:T(128)} %live_ref.1, bf16[192,16384]{1,0:T(8,128)(2,1)} %bitcast.4, bf16[192,1024]{1,0:T(8,128)(2,1)} %copy-done.1, bf16[192,1024]{1,0:T(8,128)(2,1)} %copy-done, f32[1,192]{1,0:T(1,128)} %bitcast.5, bf16[192,576]{1,0:T(8,128)(2,1)} %w_qkv.1, ...), custom_call_target="tpu_custom_call" | custom-call | tf_op jit(solution)/shard_map/pallas_call | solution.py:245
Async XLA Ops:
  1.2 10.0 %collective-permute-start.1 = (bf16[192,1024]{1,0:T(8,128)(2,1)S(1)}, bf16[192,1024]{1,0:T(8,128)(2,1)S(1)}, u32[]{:S(2)}, u32[]{:S(2)}) collective-permute-start(bf16[192,1024]{1,0:T(8,128)(2,1)S(1)} %get-tuple-element.5), channel_id=1, source_target_pairs={{1,0},{2,1},{3,2},{4,3},{5,4},{6,5},{7,6},{8,7},{9,8},{10,9},{11,1... | collective-permute-start | bytes 1179656 | tf_op jit(solution)/shard_map/ppermute | solution.py:273
  3.1 12.4 %collective-permute-start = (bf16[192,1024]{1,0:T(8,128)(2,1)S(1)}, bf16[192,1024]{1,0:T(8,128)(2,1)S(1)}, u32[]{:S(2)}, u32[]{:S(2)}) collective-permute-start(bf16[192,1024]{1,0:T(8,128)(2,1)S(1)} %get-tuple-element.6), channel_id=1, source_target_pairs={{0,1},{1,2},{2,3},{3,4},{4,5},{5,6},{6,7},{7,8},{8,9},{9,10},{10,1... | collective-permute-start | bytes 1179656 | tf_op jit(solution)/shard_map/ppermute | solution.py:272
  11.2 4.4 %copy-start = (bf16[192,1024]{1,0:T(8,128)(2,1)}, bf16[192,1024]{1,0:T(8,128)(2,1)S(1)}, u32[]{:S(2)}) copy-start(bf16[192,1024]{1,0:T(8,128)(2,1)S(1)} %collective-permute-done.1.high) | copy-start | bytes 1179652
  15.5 0.7 copy-start.1

commit v3 on v2

--- a/solution.py
+++ b/solution.py
@@ -74,7 +74,7 @@
     pipelined(BLOCK // SUB, ((norm, 0), (dot, 1), (keep, 2)))
 
 
-def attend(column, window, far_ref, xq, w_out, store, far_rows, spread):
+def attend(count, column, window, far_ref, xq, w_out, store, far_rows, spread):
     width = xq.shape[0]
     head_dim = width // HEADS
     factor = math.log2(math.e) / math.sqrt(head_dim)
@@ -156,7 +156,7 @@
 
     lags = [EARLY, PREP, AHEAD, BEHIND, TAIL]
     lags = [sum(lags[:i]) for i in range(6)]
-    pipelined(GROUP * per, tuple(zip((gather, prepare, score, softmax, blend, finish), lags)))
+    pipelined(count * per, tuple(zip((gather, prepare, score, softmax, blend, finish), lags)))
 
 
 def arrange(gain, w_qkv, w_out, full_gain, wq, wkv, wo):
@@ -173,28 +173,7 @@
     wkv[...] = jnp.concatenate(parts, axis=1).astype(wkv.dtype)
 
 
-def body(
-    far_ref, live_ref, x, low, high, gain, w_qkv, w_out, out,
-    store, xq, far_rows, spread, full_gain, wq, wkv, wo, got, sent,
-):
-    width, rows = x.shape
-    reach = low.shape[1]
-    halo, main = reach // BLOCK, rows // BLOCK
-
-    def fetch(src, at, column, size, slot):
-        return pltpu.make_async_copy(
-            src.at[:, pl.ds(at, size)], xq.at[:, pl.ds(column, size)], got.at[slot]
-        )
-
-    copies = [fetch(x, i * BLOCK, reach + i * BLOCK, BLOCK, i) for i in range(main)]
-    copies += [fetch(low, i * BLOCK, i * BLOCK, BLOCK, main + i) for i in range(halo)]
-    copies += [
-        fetch(high, i * BLOCK, reach + rows + i * BLOCK, BLOCK, main + halo + i)
-        for i in range(halo)
-    ]
-    for copy in copies:
-        copy.start()
-    arrange(gain, w_qkv, w_out, full_gain, wq, wkv, wo)
+def clear(spread):
     for slot in range(SLOTS):
         spread[slot, :, :] = jnp.zeros(spread.shape[1:], spread.dtype)
         ones = lax.broadcasted_iota(jnp.int32, (16, spread.shape[2]), 0) == 0
@@ -202,65 +181,188 @@
             spread.dtype
         )
 
-    def own_block(i, _):
-        column = pl.multiple_of(reach + i * BLOCK, BLOCK)
-        fetch(x, pl.multiple_of(i * BLOCK, BLOCK), column, BLOCK, i).wait()
+
+def inner_body(
+    group, far_ref, live_ref, x, gain, w_qkv, w_out, out, edge_rows, edge_q,
+    store, xq, far_rows, spread, full_gain, wq, wkv, wo, got, sent, kept,
+):
+    rows = x.shape[1]
+    blocks, span = rows // BLOCK, group * WIN
+    groups = (rows - 2 * REACH) // span
+
+    def fetch(i):
+        cut = pl.ds(i * BLOCK if isinstance(i, int) else pl.multiple_of(i * BLOCK, BLOCK), BLOCK)
+        return pltpu.make_async_copy(x.at[:, cut], xq.at[:, cut], got.at[i])
+
+    for i in range(blocks):
+        fetch(i).start()
+    arrange(gain, w_qkv, w_out, full_gain, wq, wkv, wo)
+    clear(spread)
+
+    def block(i, _):
+        fetch(i).wait()
         live = lambda n: live_ref[i * (BLOCK // WIN) + n]
-        project(xq, column, full_gain, wq, wkv, store, live)
+        project(xq, pl.multiple_of(i * BLOCK, BLOCK), full_gain, wq, wkv, store, live)
         return 0
 
-    lax.fori_loop(0, main, own_block, 0)
-    for i in range(2 * halo):
-        copies[main + i].wait()
-        column = i * BLOCK if i < halo else rows + i * BLOCK
-        project(xq, column, full_gain, wq, wkv, store, queries=False)
-
-    span = GROUP * WIN
+    lax.fori_loop(0, blocks, block, 0)
+    size = 2 * REACH * PARTS
+    copies = []
+    for side in range(2):
+        copies.append(
+            pltpu.make_async_copy(
+                store.at[pl.ds(PAD + side * (rows * PARTS - size), size)],
+                edge_rows.at[pl.ds(side * size, size)],
+                kept.at[side],
+            )
+        )
+        copies.append(
+            pltpu.make_async_copy(
+                xq.at[:, pl.ds(side * (rows - REACH), REACH)],
+                edge_q.at[:, pl.ds(side * REACH, REACH)],
+                kept.at[2 + side],
+            )
+        )
+    for copy in copies:
+        copy.start()
 
     def send(i):
-        at = i * span if isinstance(i, int) else pl.multiple_of(i * span, span)
-        return pltpu.make_async_copy(
-            xq.at[:, pl.ds(reach + at, span)], out.at[:, pl.ds(at, span)], sent.at[i]
-        )
-
-    def own_group(i, _):
-        column = pl.multiple_of(reach + i * span, span)
-        attend(column, i * GROUP, far_ref, xq, wo, store, far_rows, spread)
+        at = REACH + (i * span if isinstance(i, int) else pl.multiple_of(i * span, span))
+        cut = pl.ds(at, span)
+        return pltpu.make_async_copy(xq.at[:, cut], out.at[:, cut], sent.at[i])
+
+    def some(i, _):
+        column = pl.multiple_of(REACH + i * span, WIN)
+        attend(
+            group, column, REACH // WIN + i * group, far_ref, xq, wo, store, far_rows, spread
+        )
         send(i).start()
         return 0
 
-    lax.fori_loop(0, rows // span, own_group, 0)
-    for i in range(rows // span):
+    lax.fori_loop(0, groups, some, 0)
+    for i in range(groups):
         send(i).wait()
-
-
-def local(x, low, high, gain, w_qkv, w_out, counts, far):
+    for copy in copies:
+        copy.wait()
+
+
+def edge_body(
+    far_ref, inner, low, high, edge_rows, edge_q, gain, w_qkv, w_out, out,
+    store, xq, far_rows, spread, full_gain, wq, wkv, wo, got, sent,
+):
+    rows = out.shape[1]
+    count, segment = REACH // WIN, 3 * REACH
+    size = 2 * REACH * PARTS
+    halos, copies = (0, 2 * segment - REACH), []
+    for side, halo in enumerate((low, high)):
+        copies.append(
+            pltpu.make_async_copy(halo, xq.at[:, pl.ds(halos[side], REACH)], got.at[side])
+        )
+        copies.append(
+            pltpu.make_async_copy(
+                edge_q.at[:, pl.ds(side * REACH, REACH)],
+                xq.at[:, pl.ds(side * segment + REACH, REACH)],
+                got.at[2 + side],
+            )
+        )
+        copies.append(
+            pltpu.make_async_copy(
+                edge_rows.at[pl.ds(side * size, size)],
+                store.at[pl.ds(PAD + (REACH + side * 2 * REACH) * PARTS, size)],
+                got.at[4 + side],
+            )
+        )
+    for copy in copies:
+        copy.start()
+    arrange(gain, w_qkv, w_out, full_gain, wq, wkv, wo)
+    clear(spread)
+    for copy in copies[0::3]:
+        copy.wait()
+
+    def halo_block(i, _):
+        column = pl.multiple_of(i * (2 * segment - REACH), BLOCK)
+        project(xq, column, full_gain, wq, wkv, store, queries=False)
+        return 0
+
+    lax.fori_loop(0, 2, halo_block, 0)
+    for copy in copies[1::3] + copies[2::3]:
+        copy.wait()
+
+    def send(side):
+        return pltpu.make_async_copy(
+            xq.at[:, pl.ds(side * segment + REACH, REACH)],
+            out.at[:, pl.ds(side * (rows - REACH), REACH)],
+            sent.at[side],
+        )
+
+    def end(side, _):
+        column = pl.multiple_of(side * segment + REACH, WIN)
+        window = side * (rows // WIN - count)
+        attend(count, column, window, far_ref, xq, wo, store, far_rows, spread)
+        return 0
+
+    lax.fori_loop(0, 2, end, 0)
+    for side in range(2):
+        send(side).start()
+    for side in range(2):
+        send(side).wait()
+
+
+def scratch(width, total):
+    bf16 = jnp.bfloat16
+    return [
+        pltpu.VMEM((total * PARTS + 2 * PAD, LANES), jnp.float32),
+        pltpu.VMEM((width, total), bf16),
+        pltpu.VMEM((SLOTS, WIN * PARTS, LANES), jnp.float32),
+        pltpu.VMEM((SLOTS, 2 * LANES, HEADS * WIN), bf16),
+        pltpu.VMEM((width, LANES), jnp.float32),
+        pltpu.VMEM((width, width), bf16),
+        pltpu.VMEM((width, PARTS * LANES), bf16),
+        pltpu.VMEM((width, width), bf16),
+    ]
+
+
+def strip(x, halo, gain, w_qkv, w_out, counts, far):
     width, rows = x.shape
-    reach = low.shape[1]
-    total = rows + 2 * reach
-    blocks = total // BLOCK
     bf16 = jnp.bfloat16
-    any_space = pl.BlockSpec(memory_space=pl.ANY)
+    hbm = pl.BlockSpec(memory_space=pl.ANY)
     smem, vmem = pl.BlockSpec(memory_space=pltpu.SMEM), pl.BlockSpec(memory_space=pltpu.VMEM)
-    return pl.pallas_call(
-        body,
-        out_shape=jax.ShapeDtypeStruct((width, rows), bf16),
-        in_specs=[smem, smem, any_space, any_space, any_space, vmem, vmem, vmem],
-        out_specs=any_space,
-        scratch_shapes=[
-            pltpu.VMEM((total * PARTS + 2 * PAD, LANES), jnp.float32),
-            pltpu.VMEM((width, total), bf16),
-            pltpu.VMEM((SLOTS, WIN * PARTS, LANES), jnp.float32),
-            pltpu.VMEM((SLOTS, 2 * LANES, HEADS * WIN), bf16),
-            pltpu.VMEM((width, LANES), jnp.float32),
-            pltpu.VMEM((width, width), bf16),
-            pltpu.VMEM((width, PARTS * LANES), bf16),
-            pltpu.VMEM((width, width), bf16),
-            pltpu.SemaphoreType.DMA((blocks,)),
-            pltpu.SemaphoreType.DMA((rows // (GROUP * WIN),)),
+    group = math.gcd((rows - 2 * REACH) // WIN, GROUP)
+    flops = 2 * rows * width * (4 * width + 4 * WIN)
+    whole = jax.ShapeDtypeStruct((width, rows), bf16)
+    inner, edge_rows, edge_q = pl.pallas_call(
+        functools.partial(inner_body, group),
+        out_shape=(
+            whole,
+            jax.ShapeDtypeStruct((4 * REACH * PARTS, LANES), jnp.float32),
+            jax.ShapeDtypeStruct((width, 2 * REACH), bf16),
+        ),
+        in_specs=[smem, smem, hbm, vmem, vmem, vmem],
+        out_specs=(hbm, hbm, hbm),
+        scratch_shapes=scratch(width, rows)
+        + [
+            pltpu.SemaphoreType.DMA((rows // BLOCK,)),
+            pltpu.SemaphoreType.DMA(((rows - 2 * REACH) // (group * WIN),)),
+            pltpu.SemaphoreType.DMA((4,)),
         ],
         compiler_params=pltpu.CompilerParams(vmem_limit_bytes=60 << 20),
-    )(far, counts, x, low, high, gain, w_qkv, w_out)
+        cost_estimate=pl.CostEstimate(
+            flops=flops, bytes_accessed=6 * rows * width, transcendentals=2 * rows * WIN * HEADS
+        ),
+        name="inner",
+    )(far, counts, x, gain, w_qkv, w_out)
+    low, high = halo
+    return pl.pallas_call(
+        edge_body,
+        out_shape=whole,
+        in_specs=[smem, hbm, hbm, hbm, hbm, hbm, vmem, vmem, vmem],
+        out_specs=hbm,
+        input_output_aliases={1: 0},
+        scratch_shapes=scratch(width, 6 * REACH)
+        + [pltpu.SemaphoreType.DMA((6,)), pltpu.SemaphoreType.DMA((2,))],
+        compiler_params=pltpu.CompilerParams(vmem_limit_bytes=60 << 20),
+        name="edge",
+    )(far, inner, low, high, edge_rows, edge_q, gain, w_qkv, w_out)
 
 
 def shards(points, gain, w_qkv, w_out, counts, far_index):
@@ -271,7 +373,7 @@
     backward = [(i + 1, i) for i in range(count - 1)]
     low = lax.ppermute(x[:, rows - REACH :], "gx", forward)
     high = lax.ppermute(x[:, :REACH], "gx", backward)
-    return local(x, low, high, gain[None, :], w_qkv, w_out, counts, far_index).T
+    return strip(x, (low, high), gain[None, :], w_qkv, w_out, counts, far_index).T
 
 
 def solution(mesh):

time: 84.5 us -> 82.9 us (0.981)
  waiting for transfers between devices: 7.89 us -> 0.01 us
  Pallas kernels: 68 us -> 74 us
    pallas_call x1 -> x2, Pallas kernels: 68 us -> 74 us  [the longest x1 60.6 us: strip(): pl.pallas_call(functools.partial(inner_body, group), out_shape=(whole, ja...]
    ppermute x1, waiting for transfers between devices: 4.38 us -> 0.01 us  [shards(): low = lax.ppermute(x[:, rows - REACH:], 'gx', forward)]
    ppermute x1, waiting for transfers between devices: 3.52 us -> 0.01 us  [shards(): high = lax.ppermute(x[:, :REACH], 'gx', backward)]
  transfers between devices with their start and end apart: 2 -> 2, of which waited for: 2 -> 0; matrix products, arithmetic and copies ran while one was open for 0% -> 0% of each run, Pallas kernels for 0% -> 73%
where the time goes in v3:
time: 82.9 us; the launch traced here: 82.6 us
  Pallas kernels  74 us (89%)
  starting transfers between devices  6.46 us (8%)
  local copies, waits for them, and re-layouts  2.06 us (2%)
    pallas_call x1, Pallas kernels, strip(): pl.pallas_call(functools.partial(inner_body, group), out_shape=(whole, ja...  60.6 us
    pallas_call x1, Pallas kernels, strip(): pl.pallas_call(edge_body, out_shape=whole, in_specs=[smem, hbm, hbm, hbm,...  13.4 us
    ppermute x1, starting transfers between devices, shards(): low = lax.ppermute(x[:, rows - REACH:], 'gx', forward)  4.49 us
    ppermute x1, starting transfers between devices, shards(): high = lax.ppermute(x[:, :REACH], 'gx', backward)  1.97 us
  transfers between devices with their start and end apart: 2, of which 0 were waited for; matrix products, arithmetic and copies ran while one was open for 0% of the time, Pallas kernels for 73%

profile of v3, /device:TPU:1, one launch (start us, length us, event | category | flops | bytes accessed | tf_op | source)
XLA Modules:
  0.0 82.6 jit_solution(12545339046171051610)
XLA Ops:
  0.0 1.2 %fusion = (bf16[192,1024]{1,0:T(8,128)(2,1)S(1)}, bf16[192,1024]{1,0:T(8,128)(2,1)S(1)}) fusion(bf16[192,16384]{1,0:T(8,128)(2,1)} %bitcast.3), kind=kLoop, calls=%fused_computation | loop fusion | bytes 1572864 | tf_op jit(solution)/shard_map/slice | solution.py:375
  1.2 2.0 %collective-permute-start.1 = (bf16[192,1024]{1,0:T(8,128)(2,1)S(1)}, bf16[192,1024]{1,0:T(8,128)(2,1)S(1)}, u32[]{:S(2)}, u32[]{:S(2)}) collective-permute-start(bf16[192,1024]{1,0:T(8,128)(2,1)S(1)} %get-tuple-element.11), channel_id=1, source_target_pairs={{1,0},{2,1},{3,2},{4,3},{5,4},{6,5},{7,6},{8,7},{9,8},{10,9},{11,1... | collective-permute-start | bytes 1179656 | tf_op jit(solution)/shard_map/ppermute | solution.py:375
  3.1 4.5 %collective-permute-start = (bf16[192,1024]{1,0:T(8,128)(2,1)S(1)}, bf16[192,1024]{1,0:T(8,128)(2,1)S(1)}, u32[]{:S(2)}, u32[]{:S(2)}) collective-permute-start(bf16[192,1024]{1,0:T(8,128)(2,1)S(1)} %get-tuple-element.12), channel_id=1, source_target_pairs={{0,1},{1,2},{2,3},{3,4},{4,5},{5,6},{6,7},{7,8},{8,9},{9,10},{10,1... | collective-permute-start | bytes 1179656 | tf_op jit(solution)/shard_map/ppermute | solution.py:374
  7.6 60.6 %inner.1 = (bf16[192,16384]{1,0:T(8,128)(2,1)}, f32[16384,128]{1,0:T(8,128)}, bf16[192,2048]{1,0:T(8,128)(2,1)}) custom-call(s32[128,128]{1,0:T(8,128)} %far_ref.3, s32[128]{0:T(128)} %live_ref.1, bf16[192,16384]{1,0:T(8,128)(2,1)} %bitcast.4, f32[1,192]{1,0:T(1,128)} %bitcast.5, bf16[192,576]{1,0:T(8,128)(2,1)} %w_qkv.3, bf16[192,192]{1,0:T(8,128)(2,1)} %w_out.3), custom_call_target="tpu_custom_call" | custom-call | flops 8053063680 | bytes 18874368 | tf_op jit(solution)/shard_map/inner/pallas_call | solution.py:333
  68.2 0.0 collective-permute-done.1.high
  68.2 0.0 copy-start
  68.2 0.0 collective-permute-done.low
  68.2 0.0 copy-start.1
  68.2 0.7 copy-done
  69.0 0.2 copy-done.1
  69.1 13.4 %edge.1 = bf16[192,16384]{1,0:T(8,128)(2,1)} custom-call(s32[128,128]{1,0:T(8,128)} %far_ref.3, bf16[192,16384]{1,0:T(8,128)(2,1)} %get-tuple-element.8.inner, bf16[192,1024]{1,0:T(8,128)(2,1)} %copy-done.1, bf16[192,1024]{1,0:T(8,128)(2,1)} %copy-done, f32[16384,128]{1,0:T(8,128)} %get-tuple-element.9.edge_rows, ...), custom_call_target="tpu_custom_call", output_to_operand_aliasing={{}: (1, {})} | custom-call | tf_op jit(solution)/shard_map/edge/pallas_call | solution.py:355
Async XLA Ops:
  1.2 67.0 %collective-permute-start.1 = (bf16[192,1024]{1,0:T(8,128)(2,1)S(1)}, bf16[192,1024]{1,0:T(8,128)(2,1)S(1)}, u32[]{:S(2)}, u32[]{:S(2)}) collective-permute-start(bf16[192,1024]{1,0:T(8,128)(2,1)S(1)} %get-tuple-element.11), channel_id=1, source_target_pairs={{1,0},{2,1},{3,2},{4,3},{5,4},{6,5},{7,6},{8,7},{9,8},{10,9},{11,1... | collective-permute-start | bytes 1179656 | tf_op jit(solution)/shard_map/ppermute | solution.py:375
  3.1 65.1 %collective-permute-start = (bf16[192,1024]{1,0:T(8,128)(2,1)S(1)}, bf16[192,1024]{1,0:T(8,128)(2,1)S(1)}, u32[]{:S(2)}, u32[]{:S(2)}) collective-permute-start(bf16[192,1024]{1,0:T(8,128)(2,1)S(1)} %get-tuple-element.12), channel_id=1, source_target_pairs={{0,1},{1,2},{2,3},{3,4},{4,5},{5,6},{6,7},{7,8},{8,9},{9,10},{10,1... | collective-permute-start | bytes 1179656 | tf_op jit(solution)/shard_map/ppermute | solution.py:374
  68.2 0.7 copy-start
  68.2 0.9 %copy-start.1 = (bf16[192,1024]{1,0:T(8,128)(2,1)}, bf16[192,1024]{1,0:T(8,128)(2,1)S(1)}, u32[]{:S(2)}) copy-start(bf16[192,1024]{1,0:T(8,128)(2,1)S(1)} %collective-permute-done.low) | copy-start | bytes 1179652

commit v4 on v3

--- a/solution.py
+++ b/solution.py
@@ -19,6 +19,7 @@
 BLOCK = 1024
 SUB = 256
 GROUP = 16
+CHUNK = 16
 SLOTS = 4
 PAIR = 2
 EARLY, PREP, AHEAD, BEHIND, TAIL = 4, 3, 3, 3, 2
@@ -128,11 +129,20 @@
         s2 = pending.pop(n)
         halves = []
         for h in range(PAIR):
-            s = s2[:, h * WIN : (h + 1) * WIN]
-            top = jnp.max(s, axis=0, keepdims=True)
-            expo = jnp.exp2((s - top) * factor)
-            inverse = 1.0 / jnp.sum(expo, axis=0, keepdims=True)
-            halves.append((expo * inverse).astype(jnp.bfloat16))
+            head = s2[:, h * WIN : (h + 1) * WIN]
+            cut = [head[c : c + CHUNK] for c in range(0, 2 * WIN, CHUNK)]
+            top = cut[0]
+            for c in cut[1:]:
+                top = jnp.maximum(top, c)
+            top = jnp.max(top, axis=0, keepdims=True)
+            expo, total = [], 0.0
+            for c in cut:
+                e = jnp.exp2((c - top) * factor)
+                expo.append(e)
+                total = total + e
+            inverse = 1.0 / jnp.sum(total, axis=0, keepdims=True)
+            prob = [(e * inverse).astype(jnp.bfloat16) for e in expo]
+            halves.append(jnp.concatenate(prob, axis=0))
         probs[n] = jnp.concatenate(halves, axis=1)
 
     def blend(n):
@@ -182,9 +192,19 @@
         )
 
 
+def load(sems, *pairs):
+    copies = [
+        pltpu.make_async_copy(src, dst, sems.at[i]) for i, (src, dst) in enumerate(pairs)
+    ]
+    for copy in copies:
+        copy.start()
+    return copies
+
+
 def inner_body(
-    group, far_ref, live_ref, x, gain, w_qkv, w_out, out, edge_rows, edge_q,
-    store, xq, far_rows, spread, full_gain, wq, wkv, wo, got, sent, kept,
+    group, far, counts, x, gain_in, w_qkv_in, w_out_in, out, edge_rows, edge_q,
+    store, xq, far_rows, spread, full_gain, wq, wkv, wo, gain, w_qkv, w_out, far_ref,
+    loaded, live_ref, got, sent, kept,
 ):
     rows = x.shape[1]
     blocks, span = rows // BLOCK, group * WIN
@@ -194,10 +214,18 @@
         cut = pl.ds(i * BLOCK if isinstance(i, int) else pl.multiple_of(i * BLOCK, BLOCK), BLOCK)
         return pltpu.make_async_copy(x.at[:, cut], xq.at[:, cut], got.at[i])
 
+    loads = load(
+        loaded, (gain_in, gain), (w_qkv_in, w_qkv), (w_out_in, w_out), (far, far_ref),
+        (counts, live_ref),
+    )
     for i in range(blocks):
         fetch(i).start()
+    clear(spread)
+    for copy in loads[:3]:
+        copy.wait()
     arrange(gain, w_qkv, w_out, full_gain, wq, wkv, wo)
-    clear(spread)
+    for copy in loads[3:]:
+        copy.wait()
 
     def block(i, _):
         fetch(i).wait()
@@ -247,36 +275,33 @@
 
 
 def edge_body(
-    far_ref, inner, low, high, edge_rows, edge_q, gain, w_qkv, w_out, out,
-    store, xq, far_rows, spread, full_gain, wq, wkv, wo, got, sent,
+    far, inner, low, high, edge_rows, edge_q, gain_in, w_qkv_in, w_out_in, out,
+    store, xq, far_rows, spread, full_gain, wq, wkv, wo, gain, w_qkv, w_out, far_ref,
+    loaded, got, sent,
 ):
     rows = out.shape[1]
     count, segment = REACH // WIN, 3 * REACH
     size = 2 * REACH * PARTS
-    halos, copies = (0, 2 * segment - REACH), []
+    windows = rows // WIN
+    halos, rest, parts = [], [], []
     for side, halo in enumerate((low, high)):
-        copies.append(
-            pltpu.make_async_copy(halo, xq.at[:, pl.ds(halos[side], REACH)], got.at[side])
-        )
-        copies.append(
-            pltpu.make_async_copy(
-                edge_q.at[:, pl.ds(side * REACH, REACH)],
-                xq.at[:, pl.ds(side * segment + REACH, REACH)],
-                got.at[2 + side],
-            )
-        )
-        copies.append(
-            pltpu.make_async_copy(
-                edge_rows.at[pl.ds(side * size, size)],
-                store.at[pl.ds(PAD + (REACH + side * 2 * REACH) * PARTS, size)],
-                got.at[4 + side],
-            )
-        )
-    for copy in copies:
-        copy.start()
+        column = side * (2 * segment - REACH)
+        halos.append((halo, xq.at[:, pl.ds(column, REACH)]))
+        cut = pl.ds(side * (windows - count), count)
+        parts.append((far.at[cut], far_ref.at[pl.ds(side * count, count)]))
+        cut = pl.ds(side * REACH, REACH)
+        rest.append((edge_q.at[:, cut], xq.at[:, pl.ds(side * segment + REACH, REACH)]))
+        rows_at = PAD + (REACH + side * 2 * REACH) * PARTS
+        rest.append((edge_rows.at[pl.ds(side * size, size)], store.at[pl.ds(rows_at, size)]))
+    loads = load(
+        loaded, (gain_in, gain), (w_qkv_in, w_qkv), (w_out_in, w_out), *halos, *parts
+    )
+    copies = load(got, *rest)
+    clear(spread)
+    for copy in loads[:3]:
+        copy.wait()
     arrange(gain, w_qkv, w_out, full_gain, wq, wkv, wo)
-    clear(spread)
-    for copy in copies[0::3]:
+    for copy in loads[3:]:
         copy.wait()
 
     def halo_block(i, _):
@@ -285,30 +310,28 @@
         return 0
 
     lax.fori_loop(0, 2, halo_block, 0)
-    for copy in copies[1::3] + copies[2::3]:
+    for copy in copies:
         copy.wait()
 
     def send(side):
+        source = pl.multiple_of(side * segment + REACH, WIN)
+        target = pl.multiple_of(side * (rows - REACH), WIN)
         return pltpu.make_async_copy(
-            xq.at[:, pl.ds(side * segment + REACH, REACH)],
-            out.at[:, pl.ds(side * (rows - REACH), REACH)],
-            sent.at[side],
+            xq.at[:, pl.ds(source, REACH)], out.at[:, pl.ds(target, REACH)], sent.at[side]
         )
 
     def end(side, _):
         column = pl.multiple_of(side * segment + REACH, WIN)
-        window = side * (rows // WIN - count)
-        attend(count, column, window, far_ref, xq, wo, store, far_rows, spread)
+        attend(count, column, side * count, far_ref, xq, wo, store, far_rows, spread)
+        send(side).start()
         return 0
 
     lax.fori_loop(0, 2, end, 0)
     for side in range(2):
-        send(side).start()
-    for side in range(2):
         send(side).wait()
 
 
-def scratch(width, total):
+def scratch(width, total, far_rows, loads):
     bf16 = jnp.bfloat16
     return [
         pltpu.VMEM((total * PARTS + 2 * PAD, LANES), jnp.float32),
@@ -319,6 +342,11 @@
         pltpu.VMEM((width, width), bf16),
         pltpu.VMEM((width, PARTS * LANES), bf16),
         pltpu.VMEM((width, width), bf16),
+        pltpu.VMEM((1, width), jnp.float32),
+        pltpu.VMEM((width, 3 * width), bf16),
+        pltpu.VMEM((width, width), bf16),
+        pltpu.SMEM((far_rows, WIN), jnp.int32),
+        pltpu.SemaphoreType.DMA((loads,)),
     ]
 
 
@@ -326,7 +354,6 @@
     width, rows = x.shape
     bf16 = jnp.bfloat16
     hbm = pl.BlockSpec(memory_space=pl.ANY)
-    smem, vmem = pl.BlockSpec(memory_space=pltpu.SMEM), pl.BlockSpec(memory_space=pltpu.VMEM)
     group = math.gcd((rows - 2 * REACH) // WIN, GROUP)
     flops = 2 * rows * width * (4 * width + 4 * WIN)
     whole = jax.ShapeDtypeStruct((width, rows), bf16)
@@ -337,10 +364,11 @@
             jax.ShapeDtypeStruct((4 * REACH * PARTS, LANES), jnp.float32),
             jax.ShapeDtypeStruct((width, 2 * REACH), bf16),
         ),
-        in_specs=[smem, smem, hbm, vmem, vmem, vmem],
+        in_specs=[hbm] * 6,
         out_specs=(hbm, hbm, hbm),
-        scratch_shapes=scratch(width, rows)
+        scratch_shapes=scratch(width, rows, rows // WIN, 5)
         + [
+            pltpu.SMEM((rows // WIN,), jnp.int32),
             pltpu.SemaphoreType.DMA((rows // BLOCK,)),
             pltpu.SemaphoreType.DMA(((rows - 2 * REACH) // (group * WIN),)),
             pltpu.SemaphoreType.DMA((4,)),
@@ -355,11 +383,11 @@
     return pl.pallas_call(
         edge_body,
         out_shape=whole,
-        in_specs=[smem, hbm, hbm, hbm, hbm, hbm, vmem, vmem, vmem],
+        in_specs=[hbm] * 9,
         out_specs=hbm,
         input_output_aliases={1: 0},
-        scratch_shapes=scratch(width, 6 * REACH)
-        + [pltpu.SemaphoreType.DMA((6,)), pltpu.SemaphoreType.DMA((2,))],
+        scratch_shapes=scratch(width, 6 * REACH, 2 * REACH // WIN, 7)
+        + [pltpu.SemaphoreType.DMA((4,)), pltpu.SemaphoreType.DMA((2,))],
         compiler_params=pltpu.CompilerParams(vmem_limit_bytes=60 << 20),
         name="edge",
     )(far, inner, low, high, edge_rows, edge_q, gain, w_qkv, w_out)

time: 82.9 us -> 79.7 us (0.961)
  Pallas kernels: 74 us -> 71 us
    pallas_call x1, Pallas kernels: 13.4 us -> 11.5 us  [strip(): pl.pallas_call(edge_body, out_shape=whole, in_specs=[hbm] * 9, out_specs=...]
    pallas_call x1, Pallas kernels: 60.6 us -> 59.4 us  [strip(): pl.pallas_call(functools.partial(inner_body, group), out_shape=(whole, ja...]
  transfers between devices with their start and end apart: 2 -> 2, of which waited for: 0 -> 0; matrix products, arithmetic and copies ran while one was open for 0% -> 0% of each run, Pallas kernels for 73% -> 75%
where the time goes in v4:
time: 79.7 us; the launch traced here: 79.5 us
  Pallas kernels  71 us (89%)
  starting transfers between devices  6.46 us (8%)
  local copies, waits for them, and re-layouts  2.06 us (3%)
    pallas_call x1, Pallas kernels, strip(): pl.pallas_call(functools.partial(inner_body, group), out_shape=(whole, ja...  59.4 us
    pallas_call x1, Pallas kernels, strip(): pl.pallas_call(edge_body, out_shape=whole, in_specs=[hbm] * 9, out_specs=...  11.5 us
    ppermute x1, starting transfers between devices, shards(): low = lax.ppermute(x[:, rows - REACH:], 'gx', forward)  4.49 us
    ppermute x1, starting transfers between devices, shards(): high = lax.ppermute(x[:, :REACH], 'gx', backward)  1.97 us
  transfers between devices with their start and end apart: 2, of which 0 were waited for; matrix products, arithmetic and copies ran while one was open for 0% of the time, Pallas kernels for 75%

profile of v4, /device:TPU:1, one launch (start us, length us, event | category | flops | bytes accessed | tf_op | source)
XLA Modules:
  0.0 79.5 jit_solution(500598840219671433)
XLA Ops:
  0.0 1.2 %fusion = (bf16[192,1024]{1,0:T(8,128)(2,1)S(1)}, bf16[192,1024]{1,0:T(8,128)(2,1)S(1)}) fusion(bf16[192,16384]{1,0:T(8,128)(2,1)} %bitcast.3), kind=kLoop, calls=%fused_computation | loop fusion | bytes 1572864 | tf_op jit(solution)/shard_map/slice | solution.py:403
  1.2 2.0 %collective-permute-start.1 = (bf16[192,1024]{1,0:T(8,128)(2,1)S(1)}, bf16[192,1024]{1,0:T(8,128)(2,1)S(1)}, u32[]{:S(2)}, u32[]{:S(2)}) collective-permute-start(bf16[192,1024]{1,0:T(8,128)(2,1)S(1)} %get-tuple-element.11), channel_id=1, source_target_pairs={{1,0},{2,1},{3,2},{4,3},{5,4},{6,5},{7,6},{8,7},{9,8},{10,9},{11,1... | collective-permute-start | bytes 1179656 | tf_op jit(solution)/shard_map/ppermute | solution.py:403
  3.1 4.5 %collective-permute-start = (bf16[192,1024]{1,0:T(8,128)(2,1)S(1)}, bf16[192,1024]{1,0:T(8,128)(2,1)S(1)}, u32[]{:S(2)}, u32[]{:S(2)}) collective-permute-start(bf16[192,1024]{1,0:T(8,128)(2,1)S(1)} %get-tuple-element.12), channel_id=1, source_target_pairs={{0,1},{1,2},{2,3},{3,4},{4,5},{5,6},{6,7},{7,8},{8,9},{9,10},{10,1... | collective-permute-start | bytes 1179656 | tf_op jit(solution)/shard_map/ppermute | solution.py:402
  7.6 59.4 %inner.1 = (bf16[192,16384]{1,0:T(8,128)(2,1)}, f32[16384,128]{1,0:T(8,128)}, bf16[192,2048]{1,0:T(8,128)(2,1)}) custom-call(s32[128,128]{1,0:T(8,128)} %far.3, s32[128]{0:T(128)} %counts.1, bf16[192,16384]{1,0:T(8,128)(2,1)} %bitcast.4, f32[1,192]{1,0:T(1,128)} %bitcast.5, bf16[192,576]{1,0:T(8,128)(2,1)} %w_qkv_in.3, bf16[192,192]{1,0:T(8,128)(2,1)} %w_out_in.3), custom_call_target="tpu_custom_call" | custom-call | flops 8053063680 | bytes 18874368 | tf_op jit(solution)/shard_map/inner/pallas_call | solution.py:360
  67.1 0.0 collective-permute-done.1.high
  67.1 0.0 copy-start
  67.1 0.0 collective-permute-done.low
  67.1 0.0 copy-start.1
  67.1 0.7 copy-done
  67.9 0.2 copy-done.1
  68.0 11.5 %edge.1 = bf16[192,16384]{1,0:T(8,128)(2,1)} custom-call(s32[128,128]{1,0:T(8,128)} %far.3, bf16[192,16384]{1,0:T(8,128)(2,1)} %get-tuple-element.8.inner, bf16[192,1024]{1,0:T(8,128)(2,1)} %copy-done.1, bf16[192,1024]{1,0:T(8,128)(2,1)} %copy-done, f32[16384,128]{1,0:T(8,128)} %get-tuple-element.9.edge_rows, ...), custom_call_target="tpu_custom_call", output_to_operand_aliasing={{}: (1, {})} | custom-call | tf_op jit(solution)/shard_map/edge/pallas_call | solution.py:383
Async XLA Ops:
  1.2 65.9 %collective-permute-start.1 = (bf16[192,1024]{1,0:T(8,128)(2,1)S(1)}, bf16[192,1024]{1,0:T(8,128)(2,1)S(1)}, u32[]{:S(2)}, u32[]{:S(2)}) collective-permute-start(bf16[192,1024]{1,0:T(8,128)(2,1)S(1)} %get-tuple-element.11), channel_id=1, source_target_pairs={{1,0},{2,1},{3,2},{4,3},{5,4},{6,5},{7,6},{8,7},{9,8},{10,9},{11,1... | collective-permute-start | bytes 1179656 | tf_op jit(solution)/shard_map/ppermute | solution.py:403
  3.1 64.0 %collective-permute-start = (bf16[192,1024]{1,0:T(8,128)(2,1)S(1)}, bf16[192,1024]{1,0:T(8,128)(2,1)S(1)}, u32[]{:S(2)}, u32[]{:S(2)}) collective-permute-start(bf16[192,1024]{1,0:T(8,128)(2,1)S(1)} %get-tuple-element.12), channel_id=1, source_target_pairs={{0,1},{1,2},{2,3},{3,4},{4,5},{5,6},{6,7},{7,8},{8,9},{9,10},{10,1... | collective-permute-start | bytes 1179656 | tf_op jit(solution)/shard_map/ppermute | solution.py:402
  67.1 0.7 copy-start
  67.1 0.9 %copy-start.1 = (bf16[192,1024]{1,0:T(8,128)(2,1)}, bf16[192,1024]{1,0:T(8,128)(2,1)S(1)}, u32[]{:S(2)}) copy-start(bf16[192,1024]{1,0:T(8,128)(2,1)S(1)} %collective-permute-done.low) | copy-start | bytes 1179652
